TPU v7x, 32 devices: a whole 2x2x4 slice. The times are simulated.
32 devices in a mesh: seq: 16 (over z, y, x), head: 2 (over core).
Axes of the slice: x: 2, y: 2, z: 4, core: 2. Of those that a mesh axis runs over, the one named last changes fastest.
Arguments:
- x_inner: bfloat16 [2, 8192, 5120], P(None, 'seq', 'head'), may hold values from -6 to 6
- z_gate: bfloat16 [2, 8192, 5120], P(None, 'seq', 'head'), may hold values from -200 to 200
- b_input: bfloat16 [2, 8192, 128], P(None, 'seq'), may hold values from -6 to 6
- c_output: bfloat16 [2, 8192, 128], P(None, 'seq'), may hold values from -6 to 6
- step_sizes: float32 [2, 8192, 80], P(None, 'seq', 'head'), may hold values from 0.0002 to 0.2
- decay_log: float32 [80], P('head'), may hold values from -20 to 2
- skip_gain: float32 [80], P('head'), may hold values from 1 to 4
- norm_gain: float32 [5120], P('head'), may hold values from 0.5 to 1.5
- goal_pos: int32 [2, 512], P(None, 'seq'), may hold values from 0 to 8191, as said below
- goal_owner: int32 [2, 512], P(None, 'seq'), may hold values from 0 to 15, as said below
- value_w1: bfloat16 [16, 5120, 1024], P('seq', None, 'head'), may hold values from -0.078125 to 0.078125
- value_b1: float32 [16, 1024], P('seq', 'head'), may hold values from -3 to 3
- value_w2: bfloat16 [16, 1024], P('seq', 'head'), may hold values from -0.1875 to 0.1875
Outputs:
- layer_out: bfloat16 [2, 8192, 5120], P(None, 'seq', 'head')
- values: float32 [2, 512], P(None, 'seq')
Inputs may be any that keep to these rules, and one draw needn't show every extreme that they name: For every sequence s and every b, goal_pos[s, b * 32 + i] for i < 32 are distinct positions from b * 512 to (b + 1) * 512 - 1, increasing in i. `goal_owner`: among the 2 x 32 goals of the columns b * 32 to (b + 1) * 32 - 1, no expert is named more than 4 times; one expert is named exactly 4 times in every such group of columns.
All inputs are finite; a program needn't handle non-finite values.
Results may differ from a plain program's by a relative error of at most 0.0056.
Values may be sent and summed in bfloat16 or wider, within the bound.
No kernel may reach another device: no remote copies, remote signals or barrier semaphores. Data moves between devices by JAX's collectives and lax.ppermute only.
A program may use at most 384 MiB of HBM per device.

v0:
```python
import jax
import jax.numpy as jnp
from jax import lax
from jax.sharding import PartitionSpec as P

HEAD_TOTAL = 80
HEAD_DIM = 64
BLOCK = 256
CAP = 4


norm_eps = 1e-05


def carried_in(value, axis, combine, identity):
    length, index = (lax.axis_size(axis), lax.axis_index(axis))
    everything = jax.tree.map(lambda part: lax.all_gather(part, axis), value)
    start = jax.tree.map(
        lambda part, zero: jnp.broadcast_to(jnp.asarray(zero, part.dtype), part.shape),
        value,
        identity,
    )

    def hop(k, before):
        reached = k < index
        new = combine(before, jax.tree.map(lambda part: part[k], everything))
        return jax.tree.map(lambda a, b: jnp.where(reached, a, b), new, before)

    return lax.fori_loop(0, length, hop, start)


def block_parts(x_seq, b_seq, c_seq, dt_seq, decay_rates):
    length = x_seq.shape[0]
    head_count = dt_seq.shape[1]
    block_count = length // BLOCK
    x_blocks = x_seq.reshape(block_count, BLOCK, head_count, -1)
    b_blocks = b_seq.reshape(block_count, BLOCK, -1)
    c_blocks = c_seq.reshape(block_count, BLOCK, -1)
    dt_blocks = jnp.transpose(dt_seq.reshape(block_count, BLOCK, head_count), (0, 2, 1))
    cumulative = jnp.cumsum(dt_blocks * decay_rates[None, :, None], axis=2)
    end_weights = jnp.exp(cumulative[:, :, -1:] - cumulative) * dt_blocks
    x_weighted = (x_blocks * jnp.transpose(end_weights, (0, 2, 1))[..., None]).astype(jnp.bfloat16)
    states = jnp.einsum("crhp,crn->chpn", x_weighted, b_blocks, preferred_element_type=jnp.float32)
    return (x_blocks, b_blocks, c_blocks, dt_blocks, cumulative, states)


def diagonal_part(x_blocks, b_blocks, c_blocks, dt_blocks, cumulative):
    routing_scores = jnp.einsum(
        "ckn,crn->ckr", c_blocks, b_blocks, preferred_element_type=jnp.float32
    )
    positions = jnp.arange(BLOCK)
    lower_mask = positions[:, None] >= positions[None, :]
    spread = cumulative[:, :, :, None] - cumulative[:, :, None, :]
    decay_mat = jnp.exp(jnp.where(lower_mask, spread, -jnp.inf))
    weights = (routing_scores[:, None] * decay_mat * dt_blocks[:, :, None, :]).astype(jnp.bfloat16)
    return jnp.einsum("chkr,crhp->ckhp", weights, x_blocks, preferred_element_type=jnp.float32)


def chain_combine(earlier, later):
    return (earlier[0] + later[0], jnp.exp(later[0])[..., None, None] * earlier[1] + later[1])


def pick_rows(layer_seq, index_seq):
    return jnp.take(layer_seq, index_seq, axis=0)


def value_terms(full_rows, value_w1, value_b1, value_w2):
    hidden = (
        jnp.einsum("sjw,wv->sjv", full_rows, value_w1[0], preferred_element_type=jnp.float32)
        + value_b1[0]
    )
    hidden = jax.nn.gelu(hidden).astype(jnp.bfloat16)
    return jnp.einsum("sjv,v->sj", hidden, value_w2[0], preferred_element_type=jnp.float32)


def finish_values(partial_sum):
    partial_sum = lax.psum(partial_sum, "head")
    return lax.all_to_all(partial_sum, "seq", split_axis=0, concat_axis=0, tiled=True)


def body(
    x_inner,
    z_gate,
    b_input,
    c_output,
    step_sizes,
    decay_log,
    skip_gain,
    norm_gain,
    goal_pos,
    goal_owner,
    value_w1,
    value_b1,
    value_w2,
):
    decay_rates = -jnp.exp(decay_log)
    seq_count = x_inner.shape[0]
    length = x_inner.shape[1]
    stored = []
    decay_sums = []
    state_sums = []
    for seq_index in range(seq_count):
        pieces = block_parts(
            x_inner[seq_index],
            b_input[seq_index],
            c_output[seq_index],
            step_sizes[seq_index],
            decay_rates,
        )
        totals = pieces[4][:, :, -1]
        entering = [jnp.zeros_like(pieces[5][0])]
        for block_index in range(totals.shape[0]):
            entering.append(
                jnp.exp(totals[block_index])[:, None, None] * entering[-1] + pieces[5][block_index]
            )
        stored.append((pieces, totals, entering))
        decay_sums.append(jnp.sum(totals, axis=0))
        state_sums.append(entering[-1])
    summary = (jnp.stack(decay_sums), jnp.stack(state_sums))
    identity = (jnp.zeros_like(summary[0]), jnp.zeros_like(summary[1]))
    incoming = carried_in(summary, "seq", chain_combine, identity)[1]
    outputs = []
    for seq_index in range(seq_count):
        pieces, totals, entering = stored[seq_index]
        x_blocks, b_blocks, c_blocks, dt_blocks, cumulative, states = pieces
        y_diag = diagonal_part(x_blocks, b_blocks, c_blocks, dt_blocks, cumulative)
        prior = jnp.cumsum(totals, axis=0) - totals
        carried = (
            jnp.exp(prior)[:, :, None, None] * incoming[seq_index][None] + jnp.stack(entering[:-1])
        ).astype(jnp.bfloat16)
        y_off = (
            jnp.einsum("ckn,chpn->ckhp", c_blocks, carried, preferred_element_type=jnp.float32)
            * jnp.exp(jnp.transpose(cumulative, (0, 2, 1)))[..., None]
        )
        y_all = y_diag + y_off + skip_gain[None, None, :, None] * x_blocks
        outputs.append(y_all.reshape(length, -1))
    y_full = jnp.stack(outputs)
    gated_out = y_full * jax.nn.silu(z_gate.astype(jnp.float32))
    squares = lax.psum(jnp.sum(gated_out * gated_out, axis=-1), "head")
    inv_rms = lax.rsqrt(squares / (HEAD_TOTAL * HEAD_DIM) + norm_eps)
    layer_out = (gated_out * inv_rms[..., None] * norm_gain).astype(jnp.bfloat16)
    goal_dev = goal_pos.shape[1]
    local_pos = goal_pos - lax.axis_index("seq") * length
    picked_rows = jax.vmap(pick_rows)(layer_out, local_pos).reshape(seq_count * goal_dev, -1)
    owners = goal_owner.reshape(-1)
    row_ids = jnp.arange(owners.shape[0])
    same_owner = (owners[:, None] == owners[None, :]) & (row_ids[None, :] < row_ids[:, None])
    slot_rank = jnp.sum(same_owner.astype(jnp.int32), axis=1)
    slot_index = owners * CAP + slot_rank
    experts = lax.axis_size("seq")
    slot_numbers = jnp.arange(experts * CAP)
    placing = (slot_numbers[:, None] == slot_index[None, :]).astype(jnp.bfloat16)
    whole_rows = lax.all_gather(picked_rows, "head", axis=1, tiled=True)
    routed_full = (
        jnp.dot(placing, whole_rows, preferred_element_type=jnp.float32)
        .astype(jnp.bfloat16)
        .reshape(experts, CAP, -1)
    )
    returned = finish_values(
        value_terms(
            lax.all_to_all(routed_full, "seq", split_axis=0, concat_axis=0, tiled=True),
            value_w1,
            value_b1,
            value_w2,
        )
    )
    picked = jnp.take(returned.reshape(-1), slot_index)
    values = picked.reshape(seq_count, goal_dev)
    return (layer_out, values)


def solution(mesh):
    placed = (
        P(None, "seq", "head"),
        P(None, "seq", "head"),
        P(None, "seq", None),
        P(None, "seq", None),
        P(None, "seq", "head"),
        P("head"),
        P("head"),
        P("head"),
        P(None, "seq"),
        P(None, "seq"),
        P("seq", None, "head"),
        P("seq", "head"),
        P("seq", "head"),
    )
    return jax.shard_map(
        body,
        mesh=mesh,
        in_specs=placed,
        out_specs=(P(None, "seq", "head"), P(None, "seq")),
        check_vma=False,
    )
```

profile of v0, /device:TPU:0, one launch (start us, length us, event | category | flops | bytes accessed | tf_op | source)
XLA Modules:
  0.0 669.2 jit_solution(8477946099829321307)
XLA Ops:
  15.7 4.4 fusion.94
  20.0 7.5 %reshape.263 = bf16[2,256,40,64]{3,2,1,0:T(8,128)(2,1)} reshape(bf16[1,512,2560]{2,1,0:T(8,128)(2,1)} %get-tuple-element.139) | data formatting | bytes 5242880 | tf_op jit(solution)/shard_map/reshape;squeeze | solution.py:36
  27.6 6.4 copy.99
  35.2 4.4 reshape.264
  39.6 5.2 copy.107
  44.8 3.5 fusion.29
  57.8 44.9 %all-gather.2 = f32[16,2,40]{2,1,0:T(2,128)} all-gather(f32[1,2,40]{2,1,0:T(2,128)S(1)} %maximum_bitcast_fusion), channel_id=2, replica_groups=mesh['seq'=16,'head'=2] {'seq'}, dimensions={0}, use_global_device_ids=true | all-gather | bytes 5440 | tf_op jit(solution)/shard_map/all_gather | solution.py:17
  110.6 375.5 %all-gather.5.cloned.1.call-done = f32[32,40,64,128]{3,2,1,0:T(8,128)} async-done(((f32[2,40,64,128]{3,2,1,0:T(8,128)}), f32[32,40,64,128]{3,2,1,0:T(8,128)}) %all-gather.5.cloned.1.call-update) | async-done | bytes 41943056 | tf_op jit(solution)/shard_map/all_gather | solution.py:17
  486.1 48.5 %while.14 = (s32[]{:T(128)}, f32[2,40,64,128]{3,2,1,0:T(8,128)S(1)}, s32[]{:T(128)}, f32[16,2,40]{2,1,0:T(2,128)}, f32[16,2,40,64,128]{4,3,2,1,0:T(8,128)}, /*index=5*/s32[]{:T(128)}, s32[]{:T(128)}) while((s32[]{:T(128)}, f32[2,40,64,128]{3,2,1,0:T(8,128)S(1)}, s32[]{:T(128)}, f32[16,2,40]{2,1,0:T(2,128)}, ...), condition=%wide.region_8.9_spmd.clone, body=%wide.region_7.8_spmd.clone.sunk | while | flops 2621444 | bytes 7865385 | solution.py:29
  492.8 2.4 fusion.112
  498.9 2.4 fusion.112
  505.0 2.4 fusion.112
  511.0 2.4 fusion.112
  517.1 2.4 fusion.112
  526.1 2.4 fusion.112
  529.2 2.4 fusion.112
  532.2 2.4 fusion.112
  537.8 7.9 %fusion.20 = f32[2,256,40,64]{1,3,2,0:T(8,128)} fusion(bf16[2,256,40,64]{1,3,2,0:T(8,128)(2,1)S(1)} %copy-done.4, f32[2,40,64,256]{3,2,1,0:T(8,128)S(1)} %fusion.33, f32[40]{0:T(128)S(1)} %copy-done.25, f32[2,256,40]{1,2,0:T(8,128)S(1)} %copy-done.10, f32[2,40,256]{2,1,0:T(8,128)S(1)} %copy.97, f32[2,40,256]{2,1,0:T(8,128)S(1)} %copy_bitcast_fusion.1, ...), kind=kOutput, calls=%fused_computation.35 | convolution fusion | flops 703856640 | bytes 13942944 | tf_op jit(solution)/shard_map/chkr,crhp->ckhp/dot_general | solution.py:56
  545.7 8.6 %copy.124 = f32[2,256,40,64]{3,2,1,0:T(8,128)} copy(f32[2,256,40,64]{1,3,2,0:T(8,128)} %fusion.20) | data formatting | bytes 10485760 | tf_op jit(solution)/shard_map/stack;reshape | solution.py:137
  554.4 9.7 %reshape.260 = f32[1,512,2560]{2,1,0:T(8,128)} reshape(f32[2,256,40,64]{3,2,1,0:T(8,128)} %copy.124) | data formatting | bytes 10485760 | tf_op jit(solution)/shard_map/stack;reshape | solution.py:137
  566.0 7.9 %fusion.22 = f32[2,256,40,64]{1,3,2,0:T(8,128)} fusion(bf16[2,256,40,64]{1,3,2,0:T(8,128)(2,1)S(1)} %copy-done.3, f32[2,40,64,256]{3,2,1,0:T(8,128)S(1)} %fusion.34, f32[2,256,40]{1,2,0:T(8,128)S(1)} %copy-done.9, f32[40]{0:T(128)S(1)} %copy-done.25, f32[2,40,256]{2,1,0:T(8,128)S(1)} %copy.112, f32[2,40,256]{2,1,0:T(8,128)S(1)} %copy_bitcast_fusion, ...), kind=kOutput, calls=%fused_computation.37 | convolution fusion | flops 703856640 | bytes 13942944 | tf_op jit(solution)/shard_map/chkr,crhp->ckhp/dot_general | solution.py:56
  573.9 8.6 %copy.125 = f32[2,256,40,64]{3,2,1,0:T(8,128)} copy(f32[2,256,40,64]{1,3,2,0:T(8,128)} %fusion.22) | data formatting | bytes 10485760 | tf_op jit(solution)/shard_map/stack;reshape | solution.py:137
  582.5 9.6 %reshape.261 = f32[1,512,2560]{2,1,0:T(8,128)} reshape(f32[2,256,40,64]{3,2,1,0:T(8,128)} %copy.125) | data formatting | bytes 10485760 | tf_op jit(solution)/shard_map/stack;reshape | solution.py:137
  592.1 11.9 %multiply_reduce_fusion = (f32[2,512]{1,0:T(2,128)S(1)}, f32[2,512,2560]{2,1,0:T(8,128)}) fusion(bf16[2,512,2560]{2,1,0:T(8,128)(2,1)} %param.16, f32[1,512,2560]{2,1,0:T(8,128)} %reshape.261, f32[1,512,2560]{2,1,0:T(8,128)} %reshape.260), kind=kLoop, calls=%fused_computation.16 | loop fusion | flops 23591936 | bytes 26218496 | tf_op jit(solution)/shard_map/reduce_sum | solution.py:139
  604.0 2.4 psum.14
  606.4 7.3 %multiply_convert_fusion.4 = bf16[2,512,2560]{2,1,0:T(8,128)(2,1)} fusion(f32[2,512,2560]{2,1,0:T(8,128)} %get-tuple-element.134, f32[2560]{0:T(1024)S(1)} %copy-done.15, f32[2,512]{1,0:T(2,128)S(1)} %add_rsqrt_fusion), kind=kLoop, calls=%fused_computation.15 | loop fusion | flops 7864320 | bytes 15742976 | tf_op jit(solution)/shard_map/convert_element_type | solution.py:141
  619.7 3.8 all-to-all-start
  623.6 17.6 %all-to-all-done = bf16[16,4,5120]{2,1,0:T(4,128)(2,1)S(1)} async-done(((bf16[16,4,5120]{2,1,0:T(4,128)(2,1)}), bf16[16,4,5120]{2,1,0:T(4,128)(2,1)S(1)}, u32[]{:S(2)}, u32[]{:S(2)}) %all-to-all-start) | async-done | bytes 655392 | tf_op jit(solution)/shard_map/all_to_all | solution.py:161
  641.2 3.6 fusion.61
  644.8 2.5 psum.15
  647.9 4.4 all-to-all-start.1
  652.5 7.2 %all-to-all-done.1 = f32[16,1,4]{2,1,0:T(1,128)S(1)} async-done(((f32[16,1,4]{2,1,0:T(1,128)}), f32[16,1,4]{2,1,0:T(1,128)S(1)}, u32[]{:S(2)}, u32[]{:S(2)}) %all-to-all-start.1) | async-done | bytes 288 | tf_op jit(solution)/shard_map/all_to_all | solution.py:78
  (157 shorter events, 70.7 us)
Async XLA Ops:
  7.2 634.1 %copy-start = (bf16[1,512]{1,0:T(2,128)(2,1)S(1)}, bf16[1,512]{1,0:T(2,128)(2,1)}, u32[]{:S(2)}) copy-start(bf16[1,512]{1,0:T(2,128)(2,1)} %param.27) | copy-start | bytes 3076
  7.2 478.9 %all-gather.5.cloned.1.call-start = ((), (), s32[]{:S(2)}) async-start(), calls=%async_computation.2 | async-start | bytes 44564480 | tf_op jit(solution)/shard_map/all_gather | solution.py:17
  14.6 20.3 %copy-start.13 = (f32[2,40]{1,0:T(2,128)}, f32[2,40]{1,0:T(2,128)S(1)}, u32[]{:S(2)}) copy-start(f32[2,40]{1,0:T(2,128)S(1)} %get-tuple-element.122) | copy-start | bytes 964
  44.8 4.4 copy-start.2
  44.8 4.4 copy-start.19
  44.8 4.4 copy-start.20
  44.8 4.4 copy-start.21
  44.8 4.4 copy-start.22
  51.2 2.5 copy-start.14
  102.9 3.9 copy-start.26
  534.6 1.6 copy-start.6
  534.6 1.6 copy-start.16
  535.9 1.8 copy-start.4
  535.9 1.9 copy-start.8
  535.9 1.9 copy-start.10
  535.9 1.9 copy-start.11
  535.9 1.9 copy-start.25
  554.4 9.8 %copy-start.1 = (f32[40,64,128]{2,1,0:T(8,128)S(1)}, f32[40,64,128]{2,1,0:T(8,128)}, u32[]{:S(2)}) copy-start(f32[40,64,128]{2,1,0:T(8,128)} %get-tuple-element.142) | copy-start | bytes 3932164
  554.4 9.8 %copy-start.5 = (f32[1,40,64,128]{3,2,1,0:T(8,128)S(1)}, f32[1,40,64,128]{3,2,1,0:T(8,128)}, u32[]{:S(2)}) copy-start(f32[1,40,64,128]{3,2,1,0:T(8,128)} %get-tuple-element.138) | copy-start | bytes 3932164
  564.1 1.7 copy-start.3
  564.1 1.8 copy-start.7
  564.1 1.8 copy-start.9
  564.1 1.8 copy-start.12
  592.1 14.4 %copy-start.15 = (f32[2560]{0:T(1024)S(1)}, f32[2560]{0:T(1024)}, u32[]{:S(2)}) copy-start(f32[2560]{0:T(1024)} %param.22) | copy-start | bytes 30724
  606.4 9.5 %copy-start.24 = (pred[64]{0:T(512)(128)(4,1)S(1)}, pred[64]{0:T(512)(128)(4,1)}, u32[]{:S(2)}) copy-start(pred[64]{0:T(512)(128)(4,1)} %broadcast_in_dim.35) | copy-start | bytes 196
  606.4 11.9 %copy-start.23 = (s32[64]{0:T(128)S(1)}, s32[64]{0:T(128)}, u32[]{:S(2)}) copy-start(s32[64]{0:T(128)} %multiply_add_fusion) | copy-start | bytes 772
  613.7 9.8 %copy-start.17 = (s32[2,32]{1,0:T(2,128)S(1)}, s32[2,32]{1,0:T(2,128)}, u32[]{:S(2)}) copy-start(s32[2,32]{1,0:T(2,128)} %param.24) | copy-start | bytes 772
  613.7 9.9 %copy-start.27 = (s32[64]{0:T(128)S(1)}, s32[64]{0:T(128)}, u32[]{:S(2)}) copy-start(s32[64]{0:T(128)} %copy-done.26) | copy-start | bytes 772
  613.7 27.5 %copy-start.18 = (f32[1,512]{1,0:T(1,128)S(1)}, f32[1,512]{1,0:T(1,128)}, u32[]{:S(2)}) copy-start(f32[1,512]{1,0:T(1,128)} %param.26) | copy-start | bytes 6148
  619.7 21.5 %all-to-all-start = ((bf16[16,4,5120]{2,1,0:T(4,128)(2,1)}), bf16[16,4,5120]{2,1,0:T(4,128)(2,1)S(1)}, u32[]{:S(2)}, u32[]{:S(2)}) async-start(bf16[16,4,5120]{2,1,0:T(4,128)(2,1)} %reshape.226), calls=%async_computation | async-start | bytes 1310720 | tf_op jit(solution)/shard_map/all_to_all | solution.py:161
  647.9 11.7 %all-to-all-start.1 = ((f32[16,1,4]{2,1,0:T(1,128)}), f32[16,1,4]{2,1,0:T(1,128)S(1)}, u32[]{:S(2)}, u32[]{:S(2)}) async-start(f32[16,1,4]{2,1,0:T(1,128)} %copy.118), calls=%async_computation.1 | async-start | bytes 16384 | tf_op jit(solution)/shard_map/all_to_all | solution.py:78
Sparse Core Ops, SparseCore 0:
  53.2 432.8 all-gather.4
where the time goes:
time: 672 us; the launch traced here: 669 us
  waiting for transfers between devices  400 us (60%)
  local copies, waits for them, and re-layouts  89 us (13%)
  other arithmetic  76.8 us (11%)
  blocking collectives  52.1 us (8%)
  matrix products  27.9 us (4%)
  between operations  14.5 us (2%)
  starting transfers between devices  8.28 us (1%)
    all_gather x1, waiting for transfers between devices, carried_in(): everything = jax.tree.map(lambda part: lax.all_gather(part, axis), value)  375 us
    all_gather x1, blocking collectives, carried_in(): everything = jax.tree.map(lambda part: lax.all_gather(part, axis), value)  44.9 us
    select_n x16, other arithmetic, hop(): return jax.tree.map(lambda a, b: jnp.where(reached, a, b), new, before)  37.7 us
    another operation x4, local copies, waits for them, and re-layouts, body(): y_full = jnp.stack(outputs)  36.6 us
    another operation x4, local copies, waits for them, and re-layouts, block_parts(): x_blocks = x_seq.reshape(block_count, BLOCK, head_count, -1)  23.5 us
    all_to_all x1, waiting for transfers between devices, body(): lax.all_to_all(routed_full, 'seq', split_axis=0, concat_axis=0, tiled=True)  17.6 us
    dot_general x2, matrix products, diagonal_part(): jnp.einsum('chkr,crhp->ckhp', weights, x_blocks, preferred_element_type=j...  15.8 us
  transfers between devices with their start and end apart: 3, of which 3 were waited for; matrix products, arithmetic and copies ran while one was open for 2% of the time, Pallas kernels for 0%

commit v1 on v0

v1 whole, which is shorter than its diff:
```python
import functools

import jax
import jax.numpy as jnp
import numpy as np
from jax import lax
from jax.experimental import pallas as pl
from jax.experimental.pallas import tpu as pltpu
from jax.sharding import PartitionSpec as P

HEAD_TOTAL = 80
HEAD_DIM = 64
NSTATE = 128
CAP = 4
PLANES = 4
CHUNK = 128
TILE = 256
EXTRA = 128
LOG2E = 1.4426950408889634
norm_eps = 1e-05
F32 = jnp.float32
BF16 = jnp.bfloat16
HIGHEST = lax.Precision.HIGHEST


def mm(a, b):
    return jnp.dot(a, b, preferred_element_type=F32)


def lane_parts(v, heads):
    hi = v.astype(BF16)
    rest = v - hi.astype(F32)
    mid = rest.astype(BF16)
    lo = (rest - mid.astype(F32)).astype(BF16)
    lane = lax.broadcasted_iota(jnp.int32, v.shape, 1)
    return jnp.where(
        lane < heads, hi.astype(F32), jnp.where(lane < 2 * heads, mid.astype(F32), lo.astype(F32))
    ).astype(BF16)


def three(v):
    hi = v.astype(BF16).astype(F32)
    mid = (v - hi).astype(BF16).astype(F32)
    return hi, mid, v - hi - mid


def tri_mask():
    rows = lax.broadcasted_iota(jnp.int32, (CHUNK, CHUNK), 0)
    cols = lax.broadcasted_iota(jnp.int32, (CHUNK, CHUNK), 1)
    return rows >= cols


def summary_kernel(groups, heads, me, x, b, dt, rate, spread, *rest):
    outs, (cum, parts, bt, st) = rest[:groups], rest[groups:]
    step = pl.program_id(0)
    length = dt.shape[1]
    width = x.shape[2]
    rows = NSTATE // groups

    @pl.when(step == 0)
    def _():
        tri = tri_mask().astype(F32)
        before = jnp.zeros((1, 128), F32)
        for k in range(length // CHUNK):
            at = pl.ds(k * CHUNK, CHUNK)
            part = (
                jnp.dot(tri, dt[0, at, :] * rate[...], precision=HIGHEST, preferred_element_type=F32)
                + before
            )
            cum[at, :] = part
            before = part[CHUNK - 1 :, :]
            bt[:, at] = b[0, at, :].astype(F32).T.astype(BF16)
        for k in range(length // CHUNK):
            at = pl.ds(k * CHUNK, CHUNK)
            parts[at, :] = lane_parts(jnp.exp2(before - cum[at, :]) * dt[0, at, :], heads)
        hi, mid, lo = three(before)
        row = lax.broadcasted_iota(jnp.int32, (rows, EXTRA), 0)
        extra = jnp.where(row == 0, hi, jnp.where(row == 1, mid, jnp.where(row == 2, lo, 0.0)))
        for d in range(groups):
            outs[d][:, pl.ds(outs[d].shape[1] - EXTRA, EXTRA)] = extra.astype(BF16)

    for i in range(width // TILE):
        at = pl.ds(i * TILE, TILE)
        weighted = (x[0, :, at].astype(F32) * mm(parts[...], spread[:, at])).astype(BF16)
        st[:, at] = mm(bt[...], weighted)
    for d in range(groups):
        outs[d][:, pl.ds(pl.multiple_of(step * width, 128), width)] = st[
            pl.ds(pl.multiple_of((me[0] ^ d) * rows, 8), rows), :
        ].astype(BF16)


def summary(s, me, x, b, dt, rate, spread, groups):
    length, feats = x.shape[1:]
    width = 512
    heads = feats // HEAD_DIM
    return pl.pallas_call(
        functools.partial(summary_kernel, groups, heads),
        grid_spec=pltpu.PrefetchScalarGridSpec(
            num_scalar_prefetch=1,
            grid=(feats // width,),
            in_specs=[
                pl.BlockSpec((1, length, width), lambda i, m: (s, 0, i)),
                pl.BlockSpec((1, length, NSTATE), lambda i, m: (s, 0, 0)),
                pl.BlockSpec((1, length, 128), lambda i, m: (s, 0, 0)),
                pl.BlockSpec((1, 128), lambda i, m: (0, 0)),
                pl.BlockSpec((128, width), lambda i, m: (0, i)),
            ],
            out_specs=[pl.BlockSpec((NSTATE // groups, feats + EXTRA), lambda i, m: (0, 0))] * groups
            + [pl.BlockSpec((length, 128), lambda i, m: (0, 0))],
            scratch_shapes=[
                pltpu.VMEM((length, 128), BF16),
                pltpu.VMEM((NSTATE, length), BF16),
                pltpu.VMEM((NSTATE, width), F32),
            ],
        ),
        out_shape=[jax.ShapeDtypeStruct((NSTATE // groups, feats + EXTRA), BF16)] * groups
        + [jax.ShapeDtypeStruct((length, 128), F32)],
        compiler_params=pltpu.CompilerParams(vmem_limit_bytes=24 << 20),
        cost_estimate=pl.CostEstimate(flops=1_400_000_000, bytes_accessed=4_000_000, transcendentals=0),
        name="summary",
    )(me, x, b, dt, rate, spread)


def totals_of(pieces, feats):
    out = []
    for piece in pieces:
        block = piece[0:8, pl.ds(feats, EXTRA)].astype(F32)
        out.append(block[0:1] + block[1:2] + block[2:3])
    return out


def factors(totals, spread, heads, tile):
    fill = [jnp.zeros((1, 128), F32)] * (-len(totals) % 16)
    stacked = jnp.concatenate(totals + fill, axis=0)
    return mm(lane_parts(jnp.exp2(stacked), heads), spread[:, tile])


def plane_kernel(groups, heads, me, spread, *rest):
    pieces, out, ordered = rest[:groups], rest[groups], rest[groups + 1]
    feats = spread.shape[1]
    rows = out.shape[0]
    for d in range(groups):
        ordered[d] = pieces[d][...]
    views = [ordered.at[me[0] ^ p] for p in range(groups)]
    totals = totals_of(views, feats)
    for i in range(feats // TILE):
        at = pl.ds(i * TILE, TILE)
        decay = factors(totals, spread, heads, at)
        total = views[0][:, at].astype(F32)
        for p in range(1, groups):
            total = decay[p : p + 1] * total + views[p][:, at].astype(F32)
        out[:, at] = total.astype(BF16)
    hi, mid, lo = three(functools.reduce(lambda a, b: a + b, totals))
    row = lax.broadcasted_iota(jnp.int32, (rows, EXTRA), 0)
    extra = jnp.where(row == 0, hi, jnp.where(row == 1, mid, jnp.where(row == 2, lo, 0.0)))
    out[:, pl.ds(feats, EXTRA)] = extra.astype(BF16)


def plane_total(me, spread, pieces):
    groups = len(pieces)
    rows, wide = pieces[0].shape
    heads = spread.shape[1] // HEAD_DIM
    vmem = pl.BlockSpec(memory_space=pltpu.VMEM)
    return pl.pallas_call(
        functools.partial(plane_kernel, groups, heads),
        in_specs=[pl.BlockSpec(memory_space=pltpu.SMEM)] + [vmem] * (groups + 1),
        out_specs=vmem,
        out_shape=jax.ShapeDtypeStruct((rows, wide), BF16),
        scratch_shapes=[pltpu.VMEM((groups, rows, wide), BF16)],
        compiler_params=pltpu.CompilerParams(vmem_limit_bytes=16 << 20),
        cost_estimate=pl.CostEstimate(flops=10_000_000, bytes_accessed=1_500_000, transcendentals=0),
        name="plane_total",
    )(me, spread, *pieces)


def incoming_kernel(groups, hops, heads, me, spread, *rest):
    pieces, below = rest[:groups], rest[groups : groups + hops]
    outs = rest[groups + hops : 2 * groups + hops]
    ordered, results = rest[2 * groups + hops :]
    feats = spread.shape[1]
    for d in range(groups):
        ordered[d] = pieces[d][...]
    views = [ordered.at[me[0] ^ p] for p in range(groups)]
    totals = totals_of(views, feats)
    below_totals = totals_of(below, feats)
    for i in range(feats // TILE):
        at = pl.ds(i * TILE, TILE)
        decay = factors(totals + below_totals, spread, heads, at)
        state = jnp.zeros((pieces[0].shape[0], TILE), F32)
        for k in range(hops - 1, -1, -1):
            state = decay[groups + k : groups + k + 1] * state + below[k][:, at].astype(F32)
        for p in range(groups):
            results[me[0] ^ p, :, at] = state.astype(BF16)
            if p < groups - 1:
                state = decay[p : p + 1] * state + views[p][:, at].astype(F32)
    for d in range(groups):
        outs[d][...] = results[d]


def incoming_states(me, spread, pieces, below):
    groups, hops = len(pieces), len(below)
    rows, wide = pieces[0].shape
    feats = spread.shape[1]
    vmem = pl.BlockSpec(memory_space=pltpu.VMEM)
    return pl.pallas_call(
        functools.partial(incoming_kernel, groups, hops, feats // HEAD_DIM),
        in_specs=[pl.BlockSpec(memory_space=pltpu.SMEM)] + [vmem] * (1 + groups + hops),
        out_specs=[vmem] * groups,
        out_shape=[jax.ShapeDtypeStruct((rows, feats), BF16)] * groups,
        scratch_shapes=[
            pltpu.VMEM((groups, rows, wide), BF16),
            pltpu.VMEM((groups, rows, feats), BF16),
        ],
        compiler_params=pltpu.CompilerParams(vmem_limit_bytes=16 << 20),
        cost_estimate=pl.CostEstimate(flops=10_000_000, bytes_accessed=2_500_000, transcendentals=0),
        name="incoming_states",
    )(me, spread, *pieces, *below)


def local_kernel(heads, x, b, c, dt, rate, skip, spread, y, state, skip_wide):
    step = pl.program_id(0)
    feats = spread.shape[1]

    @pl.when(step == 0)
    def _():
        state[...] = jnp.zeros_like(state)
        for i in range(feats // TILE):
            at = pl.ds(i * TILE, TILE)
            skip_wide[:, at] = mm(
                lane_parts(jnp.broadcast_to(skip[...], (16, 128)), heads), spread[:, at]
            )[:8]

    keep = tri_mask()
    steps = dt[0]
    cum = jnp.dot(
        keep.astype(F32), steps * rate[...], precision=HIGHEST, preferred_element_type=F32
    )
    from_row = (cum - jnp.log2(steps)).T
    b_in, c_out = b[0], c[0]
    scores = lax.dot_general(c_out, b_in, (((1,), (1,)), ((), ())), preferred_element_type=F32)
    b_t = b_in.astype(F32).T.astype(BF16)
    grow = lane_parts(jnp.exp2(cum), heads)
    fade = lane_parts(jnp.exp2(cum[CHUNK - 1 :, :] - cum) * steps, heads)
    first = lax.broadcasted_iota(jnp.int32, (CHUNK, 128), 1) < HEAD_DIM
    nothing = jnp.zeros((CHUNK, 128), BF16)

    def weights(h):
        return jnp.where(
            keep, scores * jnp.exp2(cum[:, h : h + 1] - from_row[h : h + 1, :]), 0.0
        ).astype(BF16)

    for i in range(feats // TILE):
        at = pl.ds(i * TILE, TILE)
        grow_wide = mm(grow, spread[:, at])
        fade_wide = mm(fade, spread[:, at])
        x_in = x[0, :, at]
        x_float = x_in.astype(F32)
        old = state[:, at]
        y_tile = mm(c_out, old.astype(BF16)) * grow_wide + skip_wide[0:1, at] * x_float
        near = []
        for j in range(TILE // 128):
            h = (i * TILE + j * 128) // HEAD_DIM
            pair = x_in[:, j * 128 : (j + 1) * 128]
            near.append(
                mm(
                    jnp.concatenate([weights(h), weights(h + 1)], axis=1),
                    jnp.concatenate(
                        [jnp.where(first, pair, nothing), jnp.where(first, nothing, pair)], axis=0
                    ),
                )
            )
        y[:, at] = y_tile + jnp.concatenate(near, axis=1)
        state[:, at] = grow_wide[CHUNK - 1 :, :] * old + mm(b_t, (x_float * fade_wide).astype(BF16))


def local_part(s, x, b, c, dt, rate, skip, spread):
    length, feats = x.shape[1:]
    return pl.pallas_call(
        functools.partial(local_kernel, feats // HEAD_DIM),
        grid=(length // CHUNK,),
        in_specs=[
            pl.BlockSpec((1, CHUNK, feats), lambda i: (s, i, 0)),
            pl.BlockSpec((1, CHUNK, NSTATE), lambda i: (s, i, 0)),
            pl.BlockSpec((1, CHUNK, NSTATE), lambda i: (s, i, 0)),
            pl.BlockSpec((1, CHUNK, 128), lambda i: (s, i, 0)),
            pl.BlockSpec((1, 128), lambda i: (0, 0)),
            pl.BlockSpec((1, 128), lambda i: (0, 0)),
            pl.BlockSpec((128, feats), lambda i: (0, 0)),
        ],
        out_specs=pl.BlockSpec((CHUNK, feats), lambda i: (i, 0)),
        out_shape=jax.ShapeDtypeStruct((length, feats), F32),
        scratch_shapes=[pltpu.VMEM((NSTATE, feats), F32), pltpu.VMEM((8, feats), F32)],
        compiler_params=pltpu.CompilerParams(vmem_limit_bytes=24 << 20),
        cost_estimate=pl.CostEstimate(flops=6_000_000_000, bytes_accessed=9_000_000, transcendentals=0),
        name="local_part",
    )(x, b, c, dt, rate, skip, spread)


def gate_kernel(s, groups, heads, slots, me, *refs):
    pieces = refs[:groups]
    y, z, c, cum, gain, slot_pos, spread = refs[groups : groups + 7]
    rest = refs[groups + 7 :]
    carried = rest[:groups] if s else ()
    rest = rest[len(carried) :]
    gated, squares = rest[:2]
    sends = rest[2 : 2 + groups]
    entering, scaled, routed = rest[2 + groups :]
    step = pl.program_id(0)
    feats = spread.shape[1]
    rows = NSTATE // groups
    share = slots // groups

    @pl.when(step == 0)
    def _():
        for d in range(groups):
            entering[pl.ds(pl.multiple_of((me[0] ^ d) * rows, 8), rows), :] = pieces[d][...].astype(F32)

    grow = lane_parts(jnp.exp2(cum[...]), heads)
    c_out = c[0]
    square = jnp.zeros((CHUNK, 128), F32)
    for i in range(feats // TILE):
        at = pl.ds(i * TILE, TILE)
        far = mm(c_out, entering[:, at].astype(BF16)) * mm(grow, spread[:, at])
        half = z[0, :, at].astype(F32) * 0.5
        value = (y[:, at] + far) * (half + half * jnp.tanh(half))
        gated[:, at] = value
        scaled[:, at] = (value * gain[:, at]).astype(BF16)
        power = value * value
        for j in range(TILE // 128):
            square = square + power[:, j * 128 : (j + 1) * 128]
    total = jnp.sum(square, axis=1, keepdims=True)
    wide = jnp.broadcast_to(total, (CHUNK, 128))
    squares[pl.ds(step, 1), :] = wide.T[0:1, :]
    hi, mid, lo = three(wide)
    lane = lax.broadcasted_iota(jnp.int32, (CHUNK, EXTRA), 1)
    extra = jnp.where(lane == 0, hi, jnp.where(lane == 1, mid, jnp.where(lane == 2, lo, 0.0)))
    scaled[:, pl.ds(feats, EXTRA)] = extra.astype(BF16)
    start = (s * pl.num_programs(0) + step) * CHUNK
    here = slot_pos[...] == start + lax.broadcasted_iota(jnp.int32, (slots, CHUNK), 1)
    picked = mm(here.astype(F32).astype(BF16), scaled[...])

    @pl.when(step == 0)
    def _():
        routed[...] = picked

    @pl.when(step > 0)
    def _():
        routed[...] += picked

    @pl.when(step == pl.num_programs(0) - 1)
    def _():
        for d in range(groups):
            part = routed[pl.ds(d * share, share), :]
            if s:
                part = part + carried[d][...].astype(F32)
            sends[d][...] = part.astype(BF16)


def gate(s, me, pieces, y, z, c, cum, gain, slot_pos, spread, carried):
    length, feats = y.shape
    groups = len(pieces)
    slots = slot_pos.shape[0]
    rows = pieces[0].shape[0]
    fixed = lambda shape: pl.BlockSpec(shape, lambda i, m: (0,) * len(shape))
    send = (slots // groups, feats + EXTRA)
    return pl.pallas_call(
        functools.partial(gate_kernel, s, groups, feats // HEAD_DIM, slots),
        grid_spec=pltpu.PrefetchScalarGridSpec(
            num_scalar_prefetch=1,
            grid=(length // CHUNK,),
            in_specs=[fixed((rows, feats))] * groups
            + [
                pl.BlockSpec((CHUNK, feats), lambda i, m: (i, 0)),
                pl.BlockSpec((1, CHUNK, feats), lambda i, m: (s, i, 0)),
                pl.BlockSpec((1, CHUNK, NSTATE), lambda i, m: (s, i, 0)),
                pl.BlockSpec((CHUNK, 128), lambda i, m: (i, 0)),
                fixed((1, feats)),
                fixed((slots, 1)),
                fixed((128, feats)),
            ]
            + [fixed(send)] * len(carried),
            out_specs=[pl.BlockSpec((CHUNK, feats), lambda i, m: (i, 0)), fixed((8, 128))]
            + [fixed(send)] * groups,
            scratch_shapes=[
                pltpu.VMEM((NSTATE, feats), F32),
                pltpu.VMEM((CHUNK, feats + EXTRA), BF16),
                pltpu.VMEM((slots, feats + EXTRA), F32),
            ],
        ),
        out_shape=[jax.ShapeDtypeStruct((length, feats), F32), jax.ShapeDtypeStruct((8, 128), F32)]
        + [jax.ShapeDtypeStruct(send, BF16)] * groups,
        compiler_params=pltpu.CompilerParams(vmem_limit_bytes=32 << 20),
        cost_estimate=pl.CostEstimate(flops=1_000_000_000, bytes_accessed=15_000_000, transcendentals=0),
        name="gate",
    )(me, *pieces, y, z, c, cum, gain, slot_pos, spread, *carried)


def scale_kernel(gated, mine, other, gain, *rest):
    out = rest[-1]
    step = pl.program_id(0)
    mean = (mine[pl.ds(step, 1), :] + other[pl.ds(step, 1), :]) / (HEAD_TOTAL * HEAD_DIM)
    inv = jnp.broadcast_to(lax.rsqrt(mean + norm_eps), (CHUNK, 128)).T
    for i in range(gated.shape[1] // 128):
        at = pl.ds(i * 128, 128)
        out[0, :, at] = (gated[:, at] * inv * gain[:, at]).astype(BF16)


def scale(s, count, gated, mine, other, gain, before):
    length, feats = gated.shape
    fixed = lambda shape: pl.BlockSpec(shape, lambda i: (0,) * len(shape))
    return pl.pallas_call(
        scale_kernel,
        grid=(length // CHUNK,),
        in_specs=[
            pl.BlockSpec((CHUNK, feats), lambda i: (i, 0)),
            fixed((8, 128)),
            fixed((8, 128)),
            fixed((1, feats)),
        ]
        + [pl.BlockSpec(memory_space=pl.ANY)] * len(before),
        out_specs=pl.BlockSpec((1, CHUNK, feats), lambda i: (s, i, 0)),
        out_shape=jax.ShapeDtypeStruct((count, length, feats), BF16),
        input_output_aliases={4: 0} if before else {},
        compiler_params=pltpu.CompilerParams(vmem_limit_bytes=24 << 20),
        cost_estimate=pl.CostEstimate(flops=10_000_000, bytes_accessed=8_000_000, transcendentals=0),
        name="scale",
    )(gated, mine, other, gain, *before)


def expert_kernel(count, core, *refs):
    own, other = refs[:count], refs[count : 2 * count]
    w1, b1, w2 = refs[2 * count : 2 * count + 3]
    outs = refs[2 * count + 3 : 3 * count + 3]
    rows_a, rows_b = refs[3 * count + 3 :]
    share, wide = own[0].shape
    feats = wide - EXTRA
    for k in range(count):
        at = pl.ds(k * share, share)
        rows_a[at, :] = own[k][...]
        rows_b[at, :] = other[k][...]
    sums = jnp.zeros((count * share, 1), F32)
    for ref in (rows_a, rows_b):
        part = ref[:, pl.ds(feats, EXTRA)].astype(F32)
        lane = lax.broadcasted_iota(jnp.int32, part.shape, 1)
        sums = sums + jnp.sum(jnp.where(lane < 3, part, 0.0), axis=1, keepdims=True)
    inv = lax.rsqrt(sums / (HEAD_TOTAL * HEAD_DIM) + norm_eps)
    lower = pl.ds(pl.multiple_of(core[0] * feats, 128), feats)
    upper = pl.ds(pl.multiple_of((1 - core[0]) * feats, 128), feats)
    pre = mm(rows_a[:, pl.ds(0, feats)], w1[0, lower, :]) + mm(
        rows_b[:, pl.ds(0, feats)], w1[0, upper, :]
    )
    pre = pre * inv + b1[...]
    hidden = jax.nn.gelu(pre).astype(BF16).astype(F32)
    value = jnp.sum(hidden * w2[...].astype(F32), axis=1, keepdims=True)
    value = jnp.broadcast_to(value, (count * share, 128))
    for k in range(count):
        outs[k][...] = value[k * share : (k + 1) * share]


def expert(core, own, other, w1, b1, w2):
    count = len(own)
    share, wide = own[0].shape
    vmem = pl.BlockSpec(memory_space=pltpu.VMEM)
    return pl.pallas_call(
        functools.partial(expert_kernel, count),
        in_specs=[pl.BlockSpec(memory_space=pltpu.SMEM)] + [vmem] * (2 * count + 3),
        out_specs=[vmem] * count,
        out_shape=[jax.ShapeDtypeStruct((share, 128), F32)] * count,
        scratch_shapes=[pltpu.VMEM((count * share, wide), BF16)] * 2,
        compiler_params=pltpu.CompilerParams(vmem_limit_bytes=24 << 20),
        cost_estimate=pl.CostEstimate(flops=400_000_000, bytes_accessed=6_000_000, transcendentals=0),
        name="expert",
    )(core, *own, *other, w1, b1, w2)


def body(
    x_inner,
    z_gate,
    b_input,
    c_output,
    step_sizes,
    decay_log,
    skip_gain,
    norm_gain,
    goal_pos,
    goal_owner,
    value_w1,
    value_b1,
    value_w2,
):
    count, length, feats = x_inner.shape
    heads = step_sizes.shape[2]
    devices = lax.axis_size("seq")
    planes = PLANES
    groups = devices // planes
    index = lax.axis_index("seq")
    place, plane = index % groups, index // groups
    me = place.reshape(1).astype(jnp.int32)
    core = lax.axis_index("head").reshape(1).astype(jnp.int32)

    def permute(value, where):
        return lax.ppermute(value, "seq", where)

    def across(value, d):
        return permute(value, [(i, i ^ d) for i in range(devices)])

    def swap(value):
        return lax.ppermute(value, "head", [(0, 1), (1, 0)])

    def triple(v, fill):
        return jnp.concatenate(
            [v, v, v, jnp.full(v.shape[:-1] + (128 - 3 * heads,), fill, F32)], axis=-1
        )

    lanes = np.arange(128)
    spread = jnp.asarray(
        (lanes[:, None] % heads == np.arange(feats)[None, :] // HEAD_DIM)
        & (lanes[:, None] < 3 * heads),
        BF16,
    )
    dt = triple(step_sizes, 1.0)
    rate = triple(-jnp.exp(decay_log) * LOG2E, 0.0)[None]
    skip = triple(skip_gain, 0.0)[None]
    gain = norm_gain[None]

    goal_dev = goal_pos.shape[1]
    owners = goal_owner.reshape(-1)
    positions = (
        goal_pos - index * length + length * jnp.arange(count, dtype=jnp.int32)[:, None]
    ).reshape(-1)
    ids = jnp.arange(owners.shape[0])
    same = (owners[:, None] == owners[None, :]) & (ids[None, :] < ids[:, None])
    rank = jnp.sum(same.astype(jnp.int32), axis=1)
    slot = (((owners % groups) ^ place) * planes + ((owners // groups) ^ plane)) * CAP + rank
    slots = devices * CAP
    taken = jnp.arange(slots)[:, None] == slot[None, :]
    slot_pos = jnp.max(jnp.where(taken, positions[None, :], -1), axis=1, keepdims=True)

    summaries = [
        summary(s, me, x_inner, b_input, dt, rate, spread, groups) for s in range(count)
    ]
    locals_ = [
        local_part(s, x_inner, b_input, c_output, dt, rate, skip, spread) for s in range(count)
    ]
    gathered = [
        [own[0]] + [across(own[d], d) for d in range(1, groups)] for own in summaries
    ]
    totals = [plane_total(me, spread, pieces) for pieces in gathered]
    below = [
        [
            permute(total, [(i, i + k * groups) for i in range(devices - k * groups)])
            for k in range(1, planes)
        ]
        for total in totals
    ]
    incoming = [incoming_states(me, spread, p, t) for p, t in zip(gathered, below)]
    entering = [[own[0]] + [across(own[d], d) for d in range(1, groups)] for own in incoming]

    gated, mine, sends = [], [], ()
    for s in range(count):
        made = gate(
            s,
            me,
            entering[s],
            locals_[s],
            z_gate,
            c_output,
            summaries[s][-1],
            gain,
            slot_pos,
            spread,
            sends,
        )
        gated.append(made[0])
        mine.append(made[1])
        sends = tuple(made[2:])
    others = [swap(v) for v in mine]
    layer_out = ()
    for s in range(count):
        layer_out = (scale(s, count, gated[s], mine[s], others[s], gain, layer_out),)

    near = [sends[0]] + [across(sends[d], d) for d in range(1, groups)]
    far = [
        jnp.concatenate([v[k * CAP : (k + 1) * CAP] for v in near], axis=0) for k in range(planes)
    ]
    own = [far[0]] + [across(far[k], k * groups) for k in range(1, planes)]
    other = [swap(v) for v in own]
    answers = expert(core, own, other, value_w1, value_b1, value_w2)
    answers = [v[:, :1] for v in answers]
    back = [answers[0]] + [across(answers[k], k * groups) for k in range(1, planes)]
    table = jnp.concatenate(back, axis=1)
    table = table + swap(table)
    tables = [table] + [across(table, d) for d in range(1, groups)]
    flat = jnp.concatenate(
        [t[d * CAP : (d + 1) * CAP].T.reshape(-1) for d, t in enumerate(tables)]
    )
    values = jnp.sum(jnp.where(taken, flat[:, None], 0.0), axis=0).reshape(count, goal_dev)
    return (layer_out[0], values)


def solution(mesh):
    placed = (
        P(None, "seq", "head"),
        P(None, "seq", "head"),
        P(None, "seq", None),
        P(None, "seq", None),
        P(None, "seq", "head"),
        P("head"),
        P("head"),
        P("head"),
        P(None, "seq"),
        P(None, "seq"),
        P("seq", None, "head"),
        P("seq", "head"),
        P("seq", "head"),
    )
    return jax.shard_map(
        body,
        mesh=mesh,
        in_specs=placed,
        out_specs=(P(None, "seq", "head"), P(None, "seq")),
        check_vma=False,
    )
```

time: 672 us -> 162 us (0.24)
  waiting for transfers between devices: 400 us -> 20.4 us
  other arithmetic: 76.8 us -> 2.64 us
  local copies, waits for them, and re-layouts: 89 us -> 34.3 us
  blocking collectives: 52.1 us -> 0 us
  starting transfers between devices: 8.28 us -> 56.2 us
  Pallas kernels: 0 us -> 46.3 us
  matrix products: 27.9 us -> 0 us
  between operations: 14.5 us -> 1.08 us
    all_gather x1 -> x0, waiting for transfers between devices: 375 us -> none  [carried_in(): everything = jax.tree.map(lambda part: lax.all_gather(part, axis), value)]
    another operation x16 -> x1, local copies, waits for them, and re-layouts: 60.6 us -> 0.01 us  [the longest x4 36.6 us: body(): y_full = jnp.stack(outputs)]
    ppermute x0 -> x37, starting transfers between devices: none -> 56.2 us  [the longest x30 54.9 us: permute(): return lax.ppermute(value, 'seq', where)]
    all_gather x2 -> x0, blocking collectives: 47.2 us -> none  [the longest x1 44.9 us: carried_in(): everything = jax.tree.map(lambda part: lax.all_gather(part, axis), value)]
    pallas_call x0 -> x13, Pallas kernels: none -> 46.3 us  [the longest x2 19.4 us: local_part(): pl.pallas_call(functools.partial(local_kernel, feats // HEAD_DIM), grid=(...]
    select_n x19 -> x0, other arithmetic: 38.3 us -> none  [the longest x16 37.7 us: hop(): return jax.tree.map(lambda a, b: jnp.where(reached, a, b), new, before)]
    unnamed x56 -> x51, local copies, waits for them, and re-layouts: 1.99 us -> 32.3 us
    dot_general x10 -> x0, matrix products: 27.9 us -> none  [the longest x2 15.8 us: diagonal_part(): jnp.einsum('chkr,crhp->ckhp', weights, x_blocks, preferred_element_type=j...]
  transfers between devices with their start and end apart: 3 -> 37, of which waited for: 3 -> 12; matrix products, arithmetic and copies ran while one was open for 2% -> 1% of each run, Pallas kernels for 0% -> 23%
where the time goes in v1:
time: 162 us; the launch traced here: 161 us
  starting transfers between devices  56.2 us (35%)
  Pallas kernels  46.3 us (29%)
  local copies, waits for them, and re-layouts  34.3 us (21%)
  waiting for transfers between devices  20.4 us (13%)
  other arithmetic  2.64 us (2%)
    ppermute x30, starting transfers between devices, permute(): return lax.ppermute(value, 'seq', where)  54.9 us
    unnamed x51, local copies, waits for them, and re-layouts  32.3 us
    pallas_call x2, Pallas kernels, local_part(): pl.pallas_call(functools.partial(local_kernel, feats // HEAD_DIM), grid=(...  19.4 us
    ppermute x30, waiting for transfers between devices, permute(): return lax.ppermute(value, 'seq', where)  19.3 us
    pallas_call x2, Pallas kernels, summary(): pl.pallas_call(functools.partial(summary_kernel, groups, heads), grid_spe...  9.53 us
    pallas_call x2, Pallas kernels, gate(): pl.pallas_call(functools.partial(gate_kernel, s, groups, feats // HEAD_DI...  8.49 us
    pallas_call x2, Pallas kernels, scale(): pl.pallas_call(scale_kernel, grid=(length // CHUNK,), in_specs=[pl.BlockS...  4.73 us
  transfers between devices with their start and end apart: 37, of which 12 were waited for; matrix products, arithmetic and copies ran while one was open for 1% of the time, Pallas kernels for 23%

profile of v1, /device:TPU:0, one launch (start us, length us, event | category | flops | bytes accessed | tf_op | source)
XLA Modules:
  0.0 161.0 jit_solution(5300106825427634270)
XLA Ops:
  4.8 2.5 %copy-done.2 = bf16[2,512,2560]{2,1,0:T(8,128)(2,1)S(1)} copy-done((bf16[2,512,2560]{2,1,0:T(8,128)(2,1)S(1)}, bf16[2,512,2560]{2,1,0:T(8,128)(2,1)}, u32[]{:S(2)}) %copy-start.2) | copy-done | bytes 5242904
  8.3 4.4 %summary.3 = (bf16[32,2688]{1,0:T(8,128)(2,1)S(1)}, bf16[32,2688]{1,0:T(8,128)(2,1)S(1)}, bf16[32,2688]{1,0:T(8,128)(2,1)S(1)}, bf16[32,2688]{1,0:T(8,128)(2,1)S(1)}, f32[512,128]{1,0:T(8,128)S(1)}) custom-call(s32[1]{0:T(128)} %bitcast.me, bf16[2,512,2560]{2,1,0:T(8,128)(2,1)S(1)} %copy-done.2, bf16[2,512,128]{2,1,0:T(8,128)(2,1)S(1)} %copy-done.14, ...), custom_call_target="tpu_custom_call" | custom-call | flops 1400000000 | bytes 4000000 | tf_op jit(solution)/shard_map/summary/pallas_call | solution.py:96
  12.7 3.0 %collective-permute-start.9 = (bf16[32,2688]{1,0:T(8,128)(2,1)S(1)}, bf16[32,2688]{1,0:T(8,128)(2,1)S(1)}, u32[]{:S(2)}, u32[]{:S(2)}) collective-permute-start(bf16[32,2688]{1,0:T(8,128)(2,1)S(1)} %get-tuple-element.46), channel_id=1, source_target_pairs={{0,2},{2,0},{4,6},{6,4},{8,10},{10,8},{12,14},{14,12},{16,18},{18,... | collective-permute-start | bytes 516104 | tf_op jit(solution)/shard_map/ppermute | solution.py:502
  17.2 5.1 %summary.2 = (bf16[32,2688]{1,0:T(8,128)(2,1)S(1)}, bf16[32,2688]{1,0:T(8,128)(2,1)}, bf16[32,2688]{1,0:T(8,128)(2,1)S(1)}, bf16[32,2688]{1,0:T(8,128)(2,1)S(1)}, f32[512,128]{1,0:T(8,128)S(1)}) custom-call(s32[1]{0:T(128)} %bitcast.me, bf16[2,512,2560]{2,1,0:T(8,128)(2,1)S(1)} %copy-done.2, bf16[2,512,128]{2,1,0:T(8,128)(2,1)S(1)} %copy-done.14, ...), custom_call_target="tpu_custom_call" | custom-call | flops 1400000000 | bytes 4000000 | tf_op jit(solution)/shard_map/summary/pallas_call | solution.py:96
  22.3 1.9 %collective-permute-start = (bf16[32,2688]{1,0:T(8,128)(2,1)}, bf16[32,2688]{1,0:T(8,128)(2,1)S(1)}, u32[]{:S(2)}, u32[]{:S(2)}) collective-permute-start(bf16[32,2688]{1,0:T(8,128)(2,1)} %get-tuple-element.37), channel_id=1, source_target_pairs={{0,2},{2,0},{4,6},{6,4},{8,10},{10,8},{12,14},{14,12},{16,18},{18,... | collective-permute-start | bytes 516104 | tf_op jit(solution)/shard_map/ppermute | solution.py:502
  25.8 9.7 %local_part.3.refs_4_ = f32[512,2560]{1,0:T(8,128)S(1)} custom-call(bf16[2,512,2560]{2,1,0:T(8,128)(2,1)S(1)} %copy-done.3, bf16[2,512,128]{2,1,0:T(8,128)(2,1)S(1)} %copy-done.14, bf16[2,512,128]{2,1,0:T(8,128)(2,1)S(1)} %copy-done.15, f32[2,512,128]{2,1,0:T(8,128)S(1)} %maximum_maximum_fusion.dt, f32[1,128]{1,0:T(1,128)S(1)} %get-tuple-element.87.rate, ...), custom_call_target="tpu_custom_call" | custom-call | flops 6000000000 | bytes 9000000 | tf_op jit(solution)/shard_map/local_part/pallas_call | solution.py:278
  35.6 2.3 %copy-done.10 = f32[512,2560]{1,0:T(8,128)} copy-done((f32[512,2560]{1,0:T(8,128)}, f32[512,2560]{1,0:T(8,128)S(1)}, u32[]{:S(2)}) %copy-start.10) | copy-done | bytes 5242904
  37.9 9.7 %local_part.2.refs_4_ = f32[512,2560]{1,0:T(8,128)S(1)} custom-call(bf16[2,512,2560]{2,1,0:T(8,128)(2,1)S(1)} %copy-done.3, bf16[2,512,128]{2,1,0:T(8,128)(2,1)S(1)} %copy-done.14, bf16[2,512,128]{2,1,0:T(8,128)(2,1)S(1)} %copy-done.15, f32[2,512,128]{2,1,0:T(8,128)S(1)} %maximum_maximum_fusion.dt, f32[1,128]{1,0:T(1,128)S(1)} %get-tuple-element.87.rate, ...), custom_call_target="tpu_custom_call" | custom-call | flops 6000000000 | bytes 9000000 | tf_op jit(solution)/shard_map/local_part/pallas_call | solution.py:278
  47.6 2.3 %copy-done.8 = f32[512,2560]{1,0:T(8,128)} copy-done((f32[512,2560]{1,0:T(8,128)}, f32[512,2560]{1,0:T(8,128)S(1)}, u32[]{:S(2)}) %copy-start.8) | copy-done | bytes 5242904
  50.6 6.0 %collective-permute-start.14 = (bf16[32,2688]{1,0:T(8,128)(2,1)S(1)}, bf16[32,2688]{1,0:T(8,128)(2,1)S(1)}, u32[]{:S(2)}, u32[]{:S(2)}) collective-permute-start(bf16[32,2688]{1,0:T(8,128)(2,1)S(1)} %plane_total.3), channel_id=1, source_target_pairs={{0,24},{2,26},{4,28},{6,30},{1,25},{3,27},{5,29},{7,31}} | collective-permute-start | bytes 516104 | tf_op jit(solution)/shard_map/ppermute | solution.py:502
  57.8 2.5 %collective-permute-start.12 = (bf16[32,2688]{1,0:T(8,128)(2,1)S(1)}, bf16[32,2688]{1,0:T(8,128)(2,1)S(1)}, u32[]{:S(2)}, u32[]{:S(2)}) collective-permute-start(bf16[32,2688]{1,0:T(8,128)(2,1)S(1)} %plane_total.3), channel_id=1, source_target_pairs={{0,8},{2,10},{4,12},{6,14},{8,16},{10,18},{12,20},{14,22},{16,24},... | collective-permute-start | bytes 516104 | tf_op jit(solution)/shard_map/ppermute | solution.py:502
  63.6 2.7 %collective-permute-start.3 = (bf16[32,2688]{1,0:T(8,128)(2,1)S(1)}, bf16[32,2688]{1,0:T(8,128)(2,1)S(1)}, u32[]{:S(2)}, u32[]{:S(2)}) collective-permute-start(bf16[32,2688]{1,0:T(8,128)(2,1)S(1)} %plane_total.2), channel_id=1, source_target_pairs={{0,8},{2,10},{4,12},{6,14},{8,16},{10,18},{12,20},{14,22},{16,24},... | collective-permute-start | bytes 516104 | tf_op jit(solution)/shard_map/ppermute | solution.py:502
  66.2 2.5 %collective-permute-done.12.rest_4_ = bf16[32,2688]{1,0:T(8,128)(2,1)S(1)} collective-permute-done((bf16[32,2688]{1,0:T(8,128)(2,1)S(1)}, bf16[32,2688]{1,0:T(8,128)(2,1)S(1)}, u32[]{:S(2)}, u32[]{:S(2)}) %collective-permute-start.12) | collective-permute-done | bytes 172064 | tf_op jit(solution)/shard_map/ppermute | solution.py:502
  75.1 1.8 %collective-permute-done.3.rest_4_ = bf16[32,2688]{1,0:T(8,128)(2,1)S(1)} collective-permute-done((bf16[32,2688]{1,0:T(8,128)(2,1)S(1)}, bf16[32,2688]{1,0:T(8,128)(2,1)S(1)}, u32[]{:S(2)}, u32[]{:S(2)}) %collective-permute-start.3) | collective-permute-done | bytes 172064 | tf_op jit(solution)/shard_map/ppermute | solution.py:502
  81.9 2.5 %copy-done.4 = bf16[2,512,2560]{2,1,0:T(8,128)(2,1)S(1)} copy-done((bf16[2,512,2560]{2,1,0:T(8,128)(2,1)S(1)}, bf16[2,512,2560]{2,1,0:T(8,128)(2,1)}, u32[]{:S(2)}) %copy-start.4) | copy-done | bytes 5242904
  84.3 2.5 %copy-done.11 = f32[512,2560]{1,0:T(8,128)S(1)} copy-done((f32[512,2560]{1,0:T(8,128)S(1)}, f32[512,2560]{1,0:T(8,128)}, u32[]{:S(2)}) %copy-start.11) | copy-done | bytes 5242904
  87.7 4.2 %gate.2 = (f32[512,2560]{1,0:T(8,128)S(1)}, f32[8,128]{1,0:T(8,128)S(1)}, bf16[16,2688]{1,0:T(8,128)(2,1)S(1)}, bf16[16,2688]{1,0:T(8,128)(2,1)S(1)}, bf16[16,26...) custom-call(s32[1]{0:T(128)} %bitcast.me, bf16[32,2560]{1,0:T(8,128)(2,1)S(1)} %copy-done.17, ...), custom_call_target="tpu_custom_call" | custom-call | flops 1000000000 | bytes 15000000 | tf_op jit(solution)/shard_map/gate/pallas_call | solution.py:366
  92.0 2.3 %copy-done.12 = f32[512,2560]{1,0:T(8,128)} copy-done((f32[512,2560]{1,0:T(8,128)}, f32[512,2560]{1,0:T(8,128)S(1)}, u32[]{:S(2)}) %copy-start.12) | copy-done | bytes 5242904
  94.3 2.5 %copy-done.5 = bf16[2,512,2560]{2,1,0:T(8,128)(2,1)S(1)} copy-done((bf16[2,512,2560]{2,1,0:T(8,128)(2,1)S(1)}, bf16[2,512,2560]{2,1,0:T(8,128)(2,1)}, u32[]{:S(2)}) %copy-start.5) | copy-done | bytes 5242904
  96.8 2.5 %copy-done.9 = f32[512,2560]{1,0:T(8,128)S(1)} copy-done((f32[512,2560]{1,0:T(8,128)S(1)}, f32[512,2560]{1,0:T(8,128)}, u32[]{:S(2)}) %copy-start.9) | copy-done | bytes 5242904
  99.3 4.3 %gate.3 = (f32[512,2560]{1,0:T(8,128)S(1)}, f32[8,128]{1,0:T(8,128)S(1)}, bf16[16,2688]{1,0:T(8,128)(2,1)S(1)}, bf16[16,2688]{1,0:T(8,128)(2,1)S(1)}, bf16[16,26...) custom-call(s32[1]{0:T(128)} %bitcast.me, bf16[32,2560]{1,0:T(8,128)(2,1)S(1)} %get-tuple-element.40.refs_0_, ...), custom_call_target="tpu_custom_call" | custom-call | flops 1000000000 | bytes 15000000 | tf_op jit(solution)/shard_map/gate/pallas_call | solution.py:366
  103.6 2.4 %copy-done.6 = f32[512,2560]{1,0:T(8,128)} copy-done((f32[512,2560]{1,0:T(8,128)}, f32[512,2560]{1,0:T(8,128)S(1)}, u32[]{:S(2)}) %copy-start.6) | copy-done | bytes 5242904
  112.1 2.4 %collective-permute-done.22 = bf16[16,2688]{1,0:T(8,128)(2,1)S(1)} collective-permute-done((bf16[16,2688]{1,0:T(8,128)(2,1)S(1)}, bf16[16,2688]{1,0:T(8,128)(2,1)S(1)}, u32[]{:S(2)}, u32[]{:S(2)}) %collective-permute-start.22) | collective-permute-done | bytes 86048 | tf_op jit(solution)/shard_map/ppermute | solution.py:502
  114.6 8.9 %collective-permute-start.23 = (bf16[16,2688]{1,0:T(8,128)(2,1)S(1)}, bf16[16,2688]{1,0:T(8,128)(2,1)S(1)}, u32[]{:S(2)}, u32[]{:S(2)}) collective-permute-start(bf16[16,2688]{1,0:T(8,128)(2,1)S(1)} %pad_maximum_fusion.1), channel_id=1, source_target_pairs={{0,8},{2,10},{4,12},{6,14},{8,0},{10,2},{12,4},{14,6},{16,24},{18,... | collective-permute-start | bytes 258056 | tf_op jit(solution)/shard_map/ppermute | solution.py:502
  123.5 2.0 %collective-permute-start.24 = (bf16[16,2688]{1,0:T(8,128)(2,1)S(1)}, bf16[16,2688]{1,0:T(8,128)(2,1)S(1)}, u32[]{:S(2)}, u32[]{:S(2)}) collective-permute-start(bf16[16,2688]{1,0:T(8,128)(2,1)S(1)} %pad_maximum_fusion.2), channel_id=1, source_target_pairs={{0,16},{2,18},{4,20},{6,22},{8,24},{10,26},{12,28},{14,30},{16,0},... | collective-permute-start | bytes 258056 | tf_op jit(solution)/shard_map/ppermute | solution.py:502
  127.8 4.3 %collective-permute-done.24.refs_2_ = bf16[16,2688]{1,0:T(8,128)(2,1)S(1)} collective-permute-done((bf16[16,2688]{1,0:T(8,128)(2,1)S(1)}, bf16[16,2688]{1,0:T(8,128)(2,1)S(1)}, u32[]{:S(2)}, u32[]{:S(2)}) %collective-permute-start.24) | collective-permute-done | bytes 86048 | tf_op jit(solution)/shard_map/ppermute | solution.py:502
  133.9 2.5 %copy-done.13 = f32[512,2560]{1,0:T(8,128)S(1)} copy-done((f32[512,2560]{1,0:T(8,128)S(1)}, f32[512,2560]{1,0:T(8,128)}, u32[]{:S(2)}) %copy-start.13) | copy-done | bytes 5242904
  136.4 2.4 %scale.2.rest_0_ = bf16[2,512,2560]{2,1,0:T(8,128)(2,1)} custom-call(f32[512,2560]{1,0:T(8,128)S(1)} %copy-done.13, f32[8,128]{1,0:T(8,128)S(1)} %get-tuple-element.61.mine, f32[8,128]{1,0:T(8,128)S(1)} %collective-permute-done.19.other, f32[1,2560]{1,0:T(1,128)S(1)} %broadcast_in_dim.50.refs_8_.gain), custom_call_target="tpu_custom_call" | custom-call | flops 10000000 | bytes 8000000 | tf_op jit(solution)/shard_map/scale/pallas_call | solution.py:411
  142.1 1.8 %collective-permute-start.31 = (f32[16,1]{1,0:T(8,128)S(1)}, f32[16,1]{1,0:T(8,128)S(1)}, u32[]{:S(2)}, u32[]{:S(2)}) collective-permute-start(f32[16,1]{1,0:T(8,128)S(1)} %bitcast.23), channel_id=1, source_target_pairs={{0,16},{2,18},{4,20},{6,22},{8,24},{10,26},{12,28},{14,30},{16,0},... | collective-permute-start | bytes 200 | tf_op jit(solution)/shard_map/ppermute | solution.py:502
  146.7 2.6 %collective-permute-done.32 = f32[16,1]{1,0:T(8,128)S(1)} collective-permute-done((f32[16,1]{1,0:T(8,128)S(1)}, f32[16,1]{1,0:T(8,128)S(1)}, u32[]{:S(2)}, u32[]{:S(2)}) %collective-permute-start.32) | collective-permute-done | bytes 96 | tf_op jit(solution)/shard_map/ppermute | solution.py:502
  149.6 2.5 %copy-done.7 = f32[512,2560]{1,0:T(8,128)S(1)} copy-done((f32[512,2560]{1,0:T(8,128)S(1)}, f32[512,2560]{1,0:T(8,128)}, u32[]{:S(2)}) %copy-start.7) | copy-done | bytes 5242904
  152.0 2.4 %scale.3 = bf16[2,512,2560]{2,1,0:T(8,128)(2,1)} custom-call(f32[512,2560]{1,0:T(8,128)S(1)} %copy-done.7, f32[8,128]{1,0:T(8,128)S(1)} %get-tuple-element.59.mine, f32[8,128]{1,0:T(8,128)S(1)} %collective-permute-done.18.other, f32[1,2560]{1,0:T(1,128)S(1)} %broadcast_in_dim.50.refs_8_.gain, ...), custom_call_target="tpu_custom_call", output_to_operand_aliasing={{}: (4, {})} | custom-call | flops 10000000 | bytes 8000000 | tf_op jit(solution)/shard_map/scale/pallas_call | solution.py:411
  (147 shorter events, 48.6 us)
Async XLA Ops:
  12.7 37.3 %collective-permute-start.9 = (bf16[32,2688]{1,0:T(8,128)(2,1)S(1)}, bf16[32,2688]{1,0:T(8,128)(2,1)S(1)}, u32[]{:S(2)}, u32[]{:S(2)}) collective-permute-start(bf16[32,2688]{1,0:T(8,128)(2,1)S(1)} %get-tuple-element.46), channel_id=1, source_target_pairs={{0,2},{2,0},{4,6},{6,4},{8,10},{10,8},{12,14},{14,12},{16,18},{18,... | collective-permute-start | bytes 516104 | tf_op jit(solution)/shard_map/ppermute | solution.py:502
  15.7 34.5 %collective-permute-start.10 = (bf16[32,2688]{1,0:T(8,128)(2,1)S(1)}, bf16[32,2688]{1,0:T(8,128)(2,1)S(1)}, u32[]{:S(2)}, u32[]{:S(2)}) collective-permute-start(bf16[32,2688]{1,0:T(8,128)(2,1)S(1)} %get-tuple-element.47), channel_id=1, source_target_pairs={{0,4},{2,6},{4,0},{6,2},{8,12},{10,14},{12,8},{14,10},{16,20},{18,... | collective-permute-start | bytes 516104 | tf_op jit(solution)/shard_map/ppermute | solution.py:502
  17.2 33.0 %collective-permute-start.11 = (bf16[32,2688]{1,0:T(8,128)(2,1)S(1)}, bf16[32,2688]{1,0:T(8,128)(2,1)S(1)}, u32[]{:S(2)}, u32[]{:S(2)}) collective-permute-start(bf16[32,2688]{1,0:T(8,128)(2,1)S(1)} %get-tuple-element.48), channel_id=1, source_target_pairs={{0,6},{2,4},{4,2},{6,0},{8,14},{10,12},{12,10},{14,8},{16,22},{18,... | collective-permute-start | bytes 516104 | tf_op jit(solution)/shard_map/ppermute | solution.py:502
  22.3 35.5 %collective-permute-start = (bf16[32,2688]{1,0:T(8,128)(2,1)}, bf16[32,2688]{1,0:T(8,128)(2,1)S(1)}, u32[]{:S(2)}, u32[]{:S(2)}) collective-permute-start(bf16[32,2688]{1,0:T(8,128)(2,1)} %get-tuple-element.37), channel_id=1, source_target_pairs={{0,2},{2,0},{4,6},{6,4},{8,10},{10,8},{12,14},{14,12},{16,18},{18,... | collective-permute-start | bytes 516104 | tf_op jit(solution)/shard_map/ppermute | solution.py:502
  24.3 36.0 %collective-permute-start.1 = (bf16[32,2688]{1,0:T(8,128)(2,1)S(1)}, bf16[32,2688]{1,0:T(8,128)(2,1)S(1)}, u32[]{:S(2)}, u32[]{:S(2)}) collective-permute-start(bf16[32,2688]{1,0:T(8,128)(2,1)S(1)} %get-tuple-element.38), channel_id=1, source_target_pairs={{0,4},{2,6},{4,0},{6,2},{8,12},{10,14},{12,8},{14,10},{16,20},{18,... | collective-permute-start | bytes 516104 | tf_op jit(solution)/shard_map/ppermute | solution.py:502
  50.0 10.3 %collective-permute-start.2 = (bf16[32,2688]{1,0:T(8,128)(2,1)S(1)}, bf16[32,2688]{1,0:T(8,128)(2,1)S(1)}, u32[]{:S(2)}, u32[]{:S(2)}) collective-permute-start(bf16[32,2688]{1,0:T(8,128)(2,1)S(1)} %get-tuple-element.39), channel_id=1, source_target_pairs={{0,6},{2,4},{4,2},{6,0},{8,14},{10,12},{12,10},{14,8},{16,22},{18,... | collective-permute-start | bytes 516104 | tf_op jit(solution)/shard_map/ppermute | solution.py:502
  50.6 13.0 %collective-permute-start.14 = (bf16[32,2688]{1,0:T(8,128)(2,1)S(1)}, bf16[32,2688]{1,0:T(8,128)(2,1)S(1)}, u32[]{:S(2)}, u32[]{:S(2)}) collective-permute-start(bf16[32,2688]{1,0:T(8,128)(2,1)S(1)} %plane_total.3), channel_id=1, source_target_pairs={{0,24},{2,26},{4,28},{6,30},{1,25},{3,27},{5,29},{7,31}} | collective-permute-start | bytes 516104 | tf_op jit(solution)/shard_map/ppermute | solution.py:502
  56.5 9.7 %collective-permute-start.13 = (bf16[32,2688]{1,0:T(8,128)(2,1)S(1)}, bf16[32,2688]{1,0:T(8,128)(2,1)S(1)}, u32[]{:S(2)}, u32[]{:S(2)}) collective-permute-start(bf16[32,2688]{1,0:T(8,128)(2,1)S(1)} %plane_total.3), channel_id=1, source_target_pairs={{0,16},{2,18},{4,20},{6,22},{8,24},{10,26},{12,28},{14,30},{1,17},... | collective-permute-start | bytes 516104 | tf_op jit(solution)/shard_map/ppermute | solution.py:502
  57.8 10.9 %collective-permute-start.12 = (bf16[32,2688]{1,0:T(8,128)(2,1)S(1)}, bf16[32,2688]{1,0:T(8,128)(2,1)S(1)}, u32[]{:S(2)}, u32[]{:S(2)}) collective-permute-start(bf16[32,2688]{1,0:T(8,128)(2,1)S(1)} %plane_total.3), channel_id=1, source_target_pairs={{0,8},{2,10},{4,12},{6,14},{8,16},{10,18},{12,20},{14,22},{16,24},... | collective-permute-start | bytes 516104 | tf_op jit(solution)/shard_map/ppermute | solution.py:502
  60.6 13.0 %collective-permute-start.5 = (bf16[32,2688]{1,0:T(8,128)(2,1)S(1)}, bf16[32,2688]{1,0:T(8,128)(2,1)S(1)}, u32[]{:S(2)}, u32[]{:S(2)}) collective-permute-start(bf16[32,2688]{1,0:T(8,128)(2,1)S(1)} %plane_total.2), channel_id=1, source_target_pairs={{0,24},{2,26},{4,28},{6,30},{1,25},{3,27},{5,29},{7,31}} | collective-permute-start | bytes 516104 | tf_op jit(solution)/shard_map/ppermute | solution.py:502
  62.3 12.8 %collective-permute-start.4 = (bf16[32,2688]{1,0:T(8,128)(2,1)S(1)}, bf16[32,2688]{1,0:T(8,128)(2,1)S(1)}, u32[]{:S(2)}, u32[]{:S(2)}) collective-permute-start(bf16[32,2688]{1,0:T(8,128)(2,1)S(1)} %plane_total.2), channel_id=1, source_target_pairs={{0,16},{2,18},{4,20},{6,22},{8,24},{10,26},{12,28},{14,30},{1,17},... | collective-permute-start | bytes 516104 | tf_op jit(solution)/shard_map/ppermute | solution.py:502
  63.6 13.4 %collective-permute-start.3 = (bf16[32,2688]{1,0:T(8,128)(2,1)S(1)}, bf16[32,2688]{1,0:T(8,128)(2,1)S(1)}, u32[]{:S(2)}, u32[]{:S(2)}) collective-permute-start(bf16[32,2688]{1,0:T(8,128)(2,1)S(1)} %plane_total.2), channel_id=1, source_target_pairs={{0,8},{2,10},{4,12},{6,14},{8,16},{10,18},{12,20},{14,22},{16,24},... | collective-permute-start | bytes 516104 | tf_op jit(solution)/shard_map/ppermute | solution.py:502
  70.6 10.6 %collective-permute-start.15 = (bf16[32,2560]{1,0:T(8,128)(2,1)}, bf16[32,2560]{1,0:T(8,128)(2,1)S(1)}, u32[]{:S(2)}, u32[]{:S(2)}) collective-permute-start(bf16[32,2560]{1,0:T(8,128)(2,1)} %get-tuple-element.50), channel_id=1, source_target_pairs={{0,2},{2,0},{4,6},{6,4},{8,10},{10,8},{12,14},{14,12},{16,18},{18,... | collective-permute-start | bytes 491528 | tf_op jit(solution)/shard_map/ppermute | solution.py:502
  72.1 9.8 %collective-permute-start.16 = (bf16[32,2560]{1,0:T(8,128)(2,1)}, bf16[32,2560]{1,0:T(8,128)(2,1)S(1)}, u32[]{:S(2)}, u32[]{:S(2)}) collective-permute-start(bf16[32,2560]{1,0:T(8,128)(2,1)} %get-tuple-element.51), channel_id=1, source_target_pairs={{0,4},{2,6},{4,0},{6,2},{8,12},{10,14},{12,8},{14,10},{16,20},{18,... | collective-permute-start | bytes 491528 | tf_op jit(solution)/shard_map/ppermute | solution.py:502
  73.6 8.2 %collective-permute-start.17 = (bf16[32,2560]{1,0:T(8,128)(2,1)}, bf16[32,2560]{1,0:T(8,128)(2,1)S(1)}, u32[]{:S(2)}, u32[]{:S(2)}) collective-permute-start(bf16[32,2560]{1,0:T(8,128)(2,1)} %get-tuple-element.52), channel_id=1, source_target_pairs={{0,6},{2,4},{4,2},{6,0},{8,14},{10,12},{12,10},{14,8},{16,22},{18,... | collective-permute-start | bytes 491528 | tf_op jit(solution)/shard_map/ppermute | solution.py:502
  78.1 16.2 %collective-permute-start.6 = (bf16[32,2560]{1,0:T(8,128)(2,1)}, bf16[32,2560]{1,0:T(8,128)(2,1)S(1)}, u32[]{:S(2)}, u32[]{:S(2)}) collective-permute-start(bf16[32,2560]{1,0:T(8,128)(2,1)} %get-tuple-element.41), channel_id=1, source_target_pairs={{0,2},{2,0},{4,6},{6,4},{8,10},{10,8},{12,14},{14,12},{16,18},{18,... | collective-permute-start | bytes 491528 | tf_op jit(solution)/shard_map/ppermute | solution.py:502
  79.6 14.7 %collective-permute-start.7 = (bf16[32,2560]{1,0:T(8,128)(2,1)}, bf16[32,2560]{1,0:T(8,128)(2,1)S(1)}, u32[]{:S(2)}, u32[]{:S(2)}) collective-permute-start(bf16[32,2560]{1,0:T(8,128)(2,1)} %get-tuple-element.42), channel_id=1, source_target_pairs={{0,4},{2,6},{4,0},{6,2},{8,12},{10,14},{12,8},{14,10},{16,20},{18,... | collective-permute-start | bytes 491528 | tf_op jit(solution)/shard_map/ppermute | solution.py:502
  81.2 13.2 %collective-permute-start.8 = (bf16[32,2560]{1,0:T(8,128)(2,1)}, bf16[32,2560]{1,0:T(8,128)(2,1)S(1)}, u32[]{:S(2)}, u32[]{:S(2)}) collective-permute-start(bf16[32,2560]{1,0:T(8,128)(2,1)} %get-tuple-element.43), channel_id=1, source_target_pairs={{0,6},{2,4},{4,2},{6,0},{8,14},{10,12},{12,10},{14,8},{16,22},{18,... | collective-permute-start | bytes 491528 | tf_op jit(solution)/shard_map/ppermute | solution.py:502
  107.5 4.6 %collective-permute-start.21 = (bf16[16,2688]{1,0:T(8,128)(2,1)S(1)}, bf16[16,2688]{1,0:T(8,128)(2,1)S(1)}, u32[]{:S(2)}, u32[]{:S(2)}) collective-permute-start(bf16[16,2688]{1,0:T(8,128)(2,1)S(1)} %get-tuple-element.64), channel_id=1, source_target_pairs={{0,4},{2,6},{4,0},{6,2},{8,12},{10,14},{12,8},{14,10},{16,20},{18,... | collective-permute-start | bytes 258056 | tf_op jit(solution)/shard_map/ppermute | solution.py:502
  109.1 5.4 %collective-permute-start.22 = (bf16[16,2688]{1,0:T(8,128)(2,1)S(1)}, bf16[16,2688]{1,0:T(8,128)(2,1)S(1)}, u32[]{:S(2)}, u32[]{:S(2)}) collective-permute-start(bf16[16,2688]{1,0:T(8,128)(2,1)S(1)} %get-tuple-element.65), channel_id=1, source_target_pairs={{0,6},{2,4},{4,2},{6,0},{8,14},{10,12},{12,10},{14,8},{16,22},{18,... | collective-permute-start | bytes 258056 | tf_op jit(solution)/shard_map/ppermute | solution.py:502
  114.6 12.7 %collective-permute-start.23 = (bf16[16,2688]{1,0:T(8,128)(2,1)S(1)}, bf16[16,2688]{1,0:T(8,128)(2,1)S(1)}, u32[]{:S(2)}, u32[]{:S(2)}) collective-permute-start(bf16[16,2688]{1,0:T(8,128)(2,1)S(1)} %pad_maximum_fusion.1), channel_id=1, source_target_pairs={{0,8},{2,10},{4,12},{6,14},{8,0},{10,2},{12,4},{14,6},{16,24},{18,... | collective-permute-start | bytes 258056 | tf_op jit(solution)/shard_map/ppermute | solution.py:502
  123.5 8.6 %collective-permute-start.24 = (bf16[16,2688]{1,0:T(8,128)(2,1)S(1)}, bf16[16,2688]{1,0:T(8,128)(2,1)S(1)}, u32[]{:S(2)}, u32[]{:S(2)}) collective-permute-start(bf16[16,2688]{1,0:T(8,128)(2,1)S(1)} %pad_maximum_fusion.2), channel_id=1, source_target_pairs={{0,16},{2,18},{4,20},{6,22},{8,24},{10,26},{12,28},{14,30},{16,0},... | collective-permute-start | bytes 258056 | tf_op jit(solution)/shard_map/ppermute | solution.py:502
  125.6 6.5 %collective-permute-start.25 = (bf16[16,2688]{1,0:T(8,128)(2,1)S(1)}, bf16[16,2688]{1,0:T(8,128)(2,1)S(1)}, u32[]{:S(2)}, u32[]{:S(2)}) collective-permute-start(bf16[16,2688]{1,0:T(8,128)(2,1)S(1)} %pad_maximum_fusion.3), channel_id=1, source_target_pairs={{0,24},{2,26},{4,28},{6,30},{8,16},{10,18},{12,20},{14,22},{16,8},... | collective-permute-start | bytes 258056 | tf_op jit(solution)/shard_map/ppermute | solution.py:502
  127.2 11.6 %collective-permute-start.26 = (bf16[16,2688]{1,0:T(8,128)(2,1)S(1)}, bf16[16,2688]{1,0:T(8,128)(2,1)S(1)}, u32[]{:S(2)}, u32[]{:S(2)}) collective-permute-start(bf16[16,2688]{1,0:T(8,128)(2,1)S(1)} %pad_maximum_fusion.refs_0_), channel_id=1, source_target_pairs={{0,1},{1,0},{2,3},{3,2},{4,5},{5,4},{6,7},{7,6},{8,9},{9,8},{10,11... | collective-permute-start | bytes 258056 | tf_op jit(solution)/shard_map/ppermute | solution.py:508
  127.3 11.5 %collective-permute-start.27 = (bf16[16,2688]{1,0:T(8,128)(2,1)S(1)}, bf16[16,2688]{1,0:T(8,128)(2,1)S(1)}, u32[]{:S(2)}, u32[]{:S(2)}) collective-permute-start(bf16[16,2688]{1,0:T(8,128)(2,1)S(1)} %collective-permute-done.23.refs_1_), channel_id=1, source_target_pairs={{0,1},{1,0},{2,3},{3,2},{4,5},{5,4},{6,7},{7,6},{8,9},{9,8},{10,11... | collective-permute-start | bytes 258056 | tf_op jit(solution)/shard_map/ppermute | solution.py:508
  132.1 6.7 %collective-permute-start.28 = (bf16[16,2688]{1,0:T(8,128)(2,1)S(1)}, bf16[16,2688]{1,0:T(8,128)(2,1)S(1)}, u32[]{:S(2)}, u32[]{:S(2)}) collective-permute-start(bf16[16,2688]{1,0:T(8,128)(2,1)S(1)} %collective-permute-done.24.refs_2_), channel_id=1, source_target_pairs={{0,1},{1,0},{2,3},{3,2},{4,5},{5,4},{6,7},{7,6},{8,9},{9,8},{10,11... | collective-permute-start | bytes 258056 | tf_op jit(solution)/shard_map/ppermute | solution.py:508
  132.1 6.7 %collective-permute-start.29 = (bf16[16,2688]{1,0:T(8,128)(2,1)S(1)}, bf16[16,2688]{1,0:T(8,128)(2,1)S(1)}, u32[]{:S(2)}, u32[]{:S(2)}) collective-permute-start(bf16[16,2688]{1,0:T(8,128)(2,1)S(1)} %collective-permute-done.25.refs_3_), channel_id=1, source_target_pairs={{0,1},{1,0},{2,3},{3,2},{4,5},{5,4},{6,7},{7,6},{8,9},{9,8},{10,11... | collective-permute-start | bytes 258056 | tf_op jit(solution)/shard_map/ppermute | solution.py:508
  133.8 15.8 %collective-permute-start.18 = (f32[8,128]{1,0:T(8,128)S(1)}, f32[8,128]{1,0:T(8,128)S(1)}, u32[]{:S(2)}, u32[]{:S(2)}) collective-permute-start(f32[8,128]{1,0:T(8,128)S(1)} %get-tuple-element.59.mine), channel_id=1, source_target_pairs={{0,1},{1,0},{2,3},{3,2},{4,5},{5,4},{6,7},{7,6},{8,9},{9,8},{10,11... | collective-permute-start | bytes 12296 | tf_op jit(solution)/shard_map/ppermute | solution.py:508
  142.1 4.5 %collective-permute-start.31 = (f32[16,1]{1,0:T(8,128)S(1)}, f32[16,1]{1,0:T(8,128)S(1)}, u32[]{:S(2)}, u32[]{:S(2)}) collective-permute-start(f32[16,1]{1,0:T(8,128)S(1)} %bitcast.23), channel_id=1, source_target_pairs={{0,16},{2,18},{4,20},{6,22},{8,24},{10,26},{12,28},{14,30},{16,0},... | collective-permute-start | bytes 200 | tf_op jit(solution)/shard_map/ppermute | solution.py:502
  143.9 5.4 %collective-permute-start.32 = (f32[16,1]{1,0:T(8,128)S(1)}, f32[16,1]{1,0:T(8,128)S(1)}, u32[]{:S(2)}, u32[]{:S(2)}) collective-permute-start(f32[16,1]{1,0:T(8,128)S(1)} %bitcast.22), channel_id=1, source_target_pairs={{0,24},{2,26},{4,28},{6,30},{8,16},{10,18},{12,20},{14,22},{16,8},... | collective-permute-start | bytes 200 | tf_op jit(solution)/shard_map/ppermute | solution.py:502
  149.5 4.9 %collective-permute-start.33 = (f32[16,4]{0,1:T(4,128)S(1)}, f32[16,4]{0,1:T(4,128)S(1)}, u32[]{:S(2)}, u32[]{:S(2)}) collective-permute-start(f32[16,4]{0,1:T(4,128)S(1)} %pad_maximum_fusion.4), channel_id=1, source_target_pairs={{0,1},{1,0},{2,3},{3,2},{4,5},{5,4},{6,7},{7,6},{8,9},{9,8},{10,11... | collective-permute-start | bytes 776 | tf_op jit(solution)/shard_map/ppermute | solution.py:508
  154.4 4.5 %collective-permute-start.36 = (f32[16,4]{0,1:T(4,128)S(1)}, f32[16,4]{0,1:T(4,128)S(1)}, u32[]{:S(2)}, u32[]{:S(2)}) collective-permute-start(f32[16,4]{0,1:T(4,128)S(1)} %fusion.6), channel_id=1, source_target_pairs={{0,6},{2,4},{4,2},{6,0},{8,14},{10,12},{12,10},{14,8},{16,22},{18,... | collective-permute-start | bytes 776 | tf_op jit(solution)/shard_map/ppermute | solution.py:502
  (30 other events, 210.6 us)

commit v2 on v1

v2 whole, which is shorter than its diff:
```python
import functools

import jax
import jax.numpy as jnp
import numpy as np
from jax import lax
from jax.experimental import pallas as pl
from jax.experimental.pallas import tpu as pltpu
from jax.sharding import PartitionSpec as P

HEAD_TOTAL = 80
HEAD_DIM = 64
NSTATE = 128
CAP = 4
PLANES = 4
CHUNK = 128
TILE = 256
EXTRA = 128
LOG2E = 1.4426950408889634
norm_eps = 1e-05
F32 = jnp.float32
BF16 = jnp.bfloat16
HIGHEST = lax.Precision.HIGHEST


def mm(a, b):
    return jnp.dot(a, b, preferred_element_type=F32)


def lane_parts(v, heads):
    hi = v.astype(BF16)
    rest = v - hi.astype(F32)
    mid = rest.astype(BF16)
    lo = (rest - mid.astype(F32)).astype(BF16)
    lane = lax.broadcasted_iota(jnp.int32, v.shape, 1)
    return jnp.where(
        lane < heads, hi.astype(F32), jnp.where(lane < 2 * heads, mid.astype(F32), lo.astype(F32))
    ).astype(BF16)


def three(v):
    hi = v.astype(BF16).astype(F32)
    mid = (v - hi).astype(BF16).astype(F32)
    return hi, mid, v - hi - mid


def step_chunk(dt, k):
    part = dt[0, :, pl.ds(k * CHUNK, CHUNK)]
    fill = jnp.ones((128 - 3 * part.shape[0], CHUNK), F32)
    return jnp.concatenate([part, part, part, fill], axis=0).T


def total_rows(total, rows):
    hi, mid, lo = three(total)
    row = lax.broadcasted_iota(jnp.int32, (rows, EXTRA), 0)
    return jnp.where(
        row == 0, hi, jnp.where(row == 1, mid, jnp.where(row == 2, lo, 0.0))
    ).astype(BF16)


def tri_mask():
    rows = lax.broadcasted_iota(jnp.int32, (CHUNK, CHUNK), 0)
    cols = lax.broadcasted_iota(jnp.int32, (CHUNK, CHUNK), 1)
    return rows >= cols


def summary_kernel(groups, heads, me, x, b, dt, rate, spread, *rest):
    outs, (cum, parts, bt, st) = rest[:groups], rest[groups:]
    s, step = pl.program_id(0), pl.program_id(1)
    length = dt.shape[2]
    width = x.shape[2]
    rows = NSTATE // groups
    mine = pl.ds(pl.multiple_of(s * rows, rows), rows)

    @pl.when(step == 0)
    def _():
        tri = tri_mask().astype(F32)
        steps = [step_chunk(dt, k) for k in range(length // CHUNK)]
        before = jnp.zeros((1, 128), F32)
        for k in range(length // CHUNK):
            at = pl.ds(k * CHUNK, CHUNK)
            part = (
                jnp.dot(tri, steps[k] * rate[...], precision=HIGHEST, preferred_element_type=F32)
                + before
            )
            cum[0, at, :] = part
            before = part[CHUNK - 1 :, :]
            bt[:, at] = b[0, at, :].astype(F32).T.astype(BF16)
        for k in range(length // CHUNK):
            at = pl.ds(k * CHUNK, CHUNK)
            parts[at, :] = lane_parts(jnp.exp2(before - cum[0, at, :]) * steps[k], heads)
        extra = total_rows(before, rows)
        for d in range(groups):
            outs[d][mine, pl.ds(outs[d].shape[1] - EXTRA, EXTRA)] = extra

    for i in range(width // TILE):
        at = pl.ds(i * TILE, TILE)
        wide = spread[:, pl.ds(pl.multiple_of(step * width + i * TILE, TILE), TILE)]
        weighted = (x[0, :, at].astype(F32) * mm(parts[...], wide)).astype(BF16)
        st[:, at] = mm(bt[...], weighted)
    for d in range(groups):
        outs[d][mine, pl.ds(pl.multiple_of(step * width, 128), width)] = st[
            pl.ds(pl.multiple_of((me[0] ^ d) * rows, 8), rows), :
        ].astype(BF16)


def summary(me, x, b, dt, rate, spread, groups):
    count, length, feats = x.shape
    width = 512
    heads = feats // HEAD_DIM
    piece = (count * NSTATE // groups, feats + EXTRA)
    return pl.pallas_call(
        functools.partial(summary_kernel, groups, heads),
        grid_spec=pltpu.PrefetchScalarGridSpec(
            num_scalar_prefetch=1,
            grid=(count, feats // width),
            in_specs=[
                pl.BlockSpec((1, length, width), lambda s, i, m: (s, 0, i)),
                pl.BlockSpec((1, length, NSTATE), lambda s, i, m: (s, 0, 0)),
                pl.BlockSpec((1, heads, length), lambda s, i, m: (s, 0, 0)),
                pl.BlockSpec((1, 128), lambda s, i, m: (0, 0)),
                pl.BlockSpec(memory_space=pltpu.VMEM),
            ],
            out_specs=[pl.BlockSpec(piece, lambda s, i, m: (0, 0))] * groups
            + [pl.BlockSpec((1, length, 128), lambda s, i, m: (s, 0, 0))],
            scratch_shapes=[
                pltpu.VMEM((length, 128), BF16),
                pltpu.VMEM((NSTATE, length), BF16),
                pltpu.VMEM((NSTATE, width), F32),
            ],
        ),
        out_shape=[jax.ShapeDtypeStruct(piece, BF16)] * groups
        + [jax.ShapeDtypeStruct((count, length, 128), F32)],
        compiler_params=pltpu.CompilerParams(vmem_limit_bytes=60 << 20),
        cost_estimate=pl.CostEstimate(flops=2_800_000_000, bytes_accessed=8_000_000, transcendentals=0),
        name="summary",
    )(me, x, b, dt, rate, spread)


def totals_of(views, feats):
    out = []
    for view in views:
        block = view[0:8, pl.ds(feats, EXTRA)].astype(F32)
        out.append(block[0:1] + block[1:2] + block[2:3])
    return out


def factors(totals, spread, heads, tile):
    fill = [jnp.zeros((1, 128), F32)] * (-len(totals) % 16)
    stacked = jnp.concatenate(totals + fill, axis=0)
    return mm(lane_parts(jnp.exp2(stacked), heads), spread[:, tile])


def plane_kernel(groups, heads, count, me, spread, *rest):
    pieces, (out, ordered) = rest[:groups], rest[-2:]
    feats = spread.shape[1]
    rows = out.shape[0] // count
    for d in range(groups):
        ordered[d] = pieces[d][...].astype(F32)
    for s in range(count):
        at_rows = pl.ds(s * rows, rows)
        views = [ordered.at[me[0] ^ p, at_rows, :] for p in range(groups)]
        totals = totals_of(views, feats)
        for i in range(feats // TILE):
            at = pl.ds(i * TILE, TILE)
            decay = factors(totals, spread, heads, at)
            total = views[0][:, at]
            for p in range(1, groups):
                total = decay[p : p + 1] * total + views[p][:, at]
            out[at_rows, at] = total.astype(BF16)
        out[at_rows, pl.ds(feats, EXTRA)] = total_rows(
            functools.reduce(lambda a, b: a + b, totals), rows
        )


def plane_total(me, spread, pieces, count, after):
    groups = len(pieces)
    rows, wide = pieces[0].shape
    heads = spread.shape[1] // HEAD_DIM
    vmem = pl.BlockSpec(memory_space=pltpu.VMEM)
    return pl.pallas_call(
        functools.partial(plane_kernel, groups, heads, count),
        in_specs=[pl.BlockSpec(memory_space=pltpu.SMEM)]
        + [vmem] * (groups + 1)
        + [pl.BlockSpec(memory_space=pl.ANY)] * len(after),
        out_specs=vmem,
        out_shape=jax.ShapeDtypeStruct((rows, wide), BF16),
        scratch_shapes=[pltpu.VMEM((groups, rows, wide), F32)],
        compiler_params=pltpu.CompilerParams(vmem_limit_bytes=12 << 20),
        cost_estimate=pl.CostEstimate(flops=10_000_000, bytes_accessed=1_500_000, transcendentals=0),
        name="plane_total",
    )(me, spread, *pieces, *after)


def incoming_kernel(groups, hops, heads, count, me, spread, *rest):
    pieces, below = rest[:groups], rest[groups : groups + hops]
    outs = rest[-groups - 2 : -2]
    ordered, results = rest[-2:]
    feats = spread.shape[1]
    rows = outs[0].shape[0] // count
    for d in range(groups):
        ordered[d] = pieces[d][...].astype(F32)
    for s in range(count):
        at_rows = pl.ds(s * rows, rows)
        views = [ordered.at[me[0] ^ p, at_rows, :] for p in range(groups)]
        under = [ref.at[at_rows, :] for ref in below]
        totals = totals_of(views, feats) + totals_of(under, feats)
        for i in range(feats // TILE):
            at = pl.ds(i * TILE, TILE)
            decay = factors(totals, spread, heads, at)
            state = jnp.zeros((rows, TILE), F32)
            for k in range(hops - 1, -1, -1):
                state = decay[groups + k : groups + k + 1] * state + under[k][:, at].astype(F32)
            for p in range(groups):
                results[me[0] ^ p, at_rows, at] = state
                if p < groups - 1:
                    state = decay[p : p + 1] * state + views[p][:, at]
    for d in range(groups):
        outs[d][...] = results[d].astype(BF16)


def incoming_states(me, spread, pieces, below, count, after):
    groups, hops = len(pieces), len(below)
    rows, wide = pieces[0].shape
    feats = spread.shape[1]
    vmem = pl.BlockSpec(memory_space=pltpu.VMEM)
    return pl.pallas_call(
        functools.partial(incoming_kernel, groups, hops, feats // HEAD_DIM, count),
        in_specs=[pl.BlockSpec(memory_space=pltpu.SMEM)]
        + [vmem] * (1 + groups + hops)
        + [pl.BlockSpec(memory_space=pl.ANY)] * len(after),
        out_specs=[vmem] * groups,
        out_shape=[jax.ShapeDtypeStruct((rows, feats), BF16)] * groups,
        scratch_shapes=[
            pltpu.VMEM((groups, rows, wide), F32),
            pltpu.VMEM((groups, rows, feats), F32),
        ],
        compiler_params=pltpu.CompilerParams(vmem_limit_bytes=14 << 20),
        cost_estimate=pl.CostEstimate(flops=10_000_000, bytes_accessed=2_500_000, transcendentals=0),
        name="incoming_states",
    )(me, spread, *pieces, *below, *after)


def local_kernel(heads, first_head, x, b, c, dt, rate, skip, spread, *rest):
    y, token, state, skip_wide = rest[-4:]
    step = pl.program_id(0)
    feats = x.shape[2]
    offset = first_head * HEAD_DIM

    @pl.when(step == 0)
    def _():
        state[...] = jnp.zeros_like(state)
        token[...] = jnp.zeros_like(token)
        for i in range(feats // TILE):
            at = pl.ds(i * TILE, TILE)
            skip_wide[:, at] = mm(
                lane_parts(jnp.broadcast_to(skip[...], (16, 128)), heads),
                spread[:, pl.ds(offset + i * TILE, TILE)],
            )[:8]

    keep = tri_mask()
    steps = step_chunk(dt, 0)
    cum = jnp.dot(
        keep.astype(F32), steps * rate[...], precision=HIGHEST, preferred_element_type=F32
    )
    from_row = (cum - jnp.log2(steps)).T
    b_in, c_out = b[0], c[0]
    scores = lax.dot_general(c_out, b_in, (((1,), (1,)), ((), ())), preferred_element_type=F32)
    b_t = b_in.astype(F32).T.astype(BF16)
    grow = lane_parts(jnp.exp2(cum), heads)
    fade = lane_parts(jnp.exp2(cum[CHUNK - 1 :, :] - cum) * steps, heads)
    first = lax.broadcasted_iota(jnp.int32, (CHUNK, 128), 1) < HEAD_DIM
    nothing = jnp.zeros((CHUNK, 128), BF16)

    def weights(h):
        return jnp.where(
            keep, scores * jnp.exp2(cum[:, h : h + 1] - from_row[h : h + 1, :]), 0.0
        ).astype(BF16)

    for i in range(feats // TILE):
        at = pl.ds(i * TILE, TILE)
        wide = spread[:, pl.ds(offset + i * TILE, TILE)]
        grow_wide = mm(grow, wide)
        fade_wide = mm(fade, wide)
        x_in = x[0, :, at]
        x_float = x_in.astype(F32)
        old = state[:, at]
        y_tile = mm(c_out, old.astype(BF16)) * grow_wide + skip_wide[0:1, at] * x_float
        near = []
        for j in range(TILE // 128):
            h = first_head + (i * TILE + j * 128) // HEAD_DIM
            pair = x_in[:, j * 128 : (j + 1) * 128]
            near.append(
                mm(
                    jnp.concatenate([weights(h), weights(h + 1)], axis=1),
                    jnp.concatenate(
                        [jnp.where(first, pair, nothing), jnp.where(first, nothing, pair)], axis=0
                    ),
                )
            )
        y[0, :, at] = (y_tile + jnp.concatenate(near, axis=1)).astype(BF16)
        state[:, at] = grow_wide[CHUNK - 1 :, :] * old + mm(b_t, (x_float * fade_wide).astype(BF16))


def local_part(s, part, parts, x, b, c, dt, rate, skip, spread, before, after):
    count, length, feats = x.shape[0], x.shape[1], x.shape[2] // parts
    heads = x.shape[2] // HEAD_DIM
    return pl.pallas_call(
        functools.partial(local_kernel, heads, part * feats // HEAD_DIM),
        grid=(length // CHUNK,),
        in_specs=[
            pl.BlockSpec((1, CHUNK, feats), lambda i: (s, i, part)),
            pl.BlockSpec((1, CHUNK, NSTATE), lambda i: (s, i, 0)),
            pl.BlockSpec((1, CHUNK, NSTATE), lambda i: (s, i, 0)),
            pl.BlockSpec((1, heads, CHUNK), lambda i: (s, 0, i)),
            pl.BlockSpec((1, 128), lambda i: (0, 0)),
            pl.BlockSpec((1, 128), lambda i: (0, 0)),
            pl.BlockSpec(memory_space=pltpu.VMEM),
        ]
        + [pl.BlockSpec(memory_space=pl.ANY)] * (len(before) + len(after)),
        out_specs=[
            pl.BlockSpec((1, CHUNK, feats), lambda i: (s, i, part)),
            pl.BlockSpec((8, 128), lambda i: (0, 0)),
        ],
        out_shape=[
            jax.ShapeDtypeStruct((count, length, feats * parts), BF16),
            jax.ShapeDtypeStruct((8, 128), F32),
        ],
        input_output_aliases={7: 0} if before else {},
        scratch_shapes=[pltpu.VMEM((NSTATE, feats), F32), pltpu.VMEM((8, feats), F32)],
        compiler_params=pltpu.CompilerParams(vmem_limit_bytes=60 << 20),
        cost_estimate=pl.CostEstimate(flops=6_000_000_000, bytes_accessed=9_000_000, transcendentals=0),
        name="local_part",
    )(x, b, c, dt, rate, skip, spread, *before, *after)


def gate_kernel(groups, heads, slots, me, *refs):
    pieces, refs = refs[:groups], refs[groups:]
    y, z, c, cum, gain, slot_pos, spread = refs[:7]
    gated, squares = refs[7:9]
    sends = refs[9 : 9 + groups]
    entering, routed = refs[9 + groups :]
    s, step = pl.program_id(0), pl.program_id(1)
    feats = spread.shape[1]
    rows = NSTATE // groups
    share = slots // groups
    row = s * pl.num_programs(1) + step

    @pl.when(step == 0)
    def _():
        mine = pl.ds(pl.multiple_of(s * rows, 8), rows)
        for d in range(groups):
            entering[pl.ds(pl.multiple_of((me[0] ^ d) * rows, 8), rows), :] = pieces[d][
                mine, :
            ].astype(F32)

    @pl.when(row == 0)
    def _():
        routed[...] = jnp.zeros_like(routed)

    grow = lane_parts(jnp.exp2(cum[0]), heads)
    c_out = c[0]
    square = jnp.zeros((CHUNK, 128), F32)
    here = slot_pos[...] == row * CHUNK + lax.broadcasted_iota(jnp.int32, (slots, CHUNK), 1)
    pick = here.astype(F32).astype(BF16)
    for i in range(feats // TILE):
        at = pl.ds(i * TILE, TILE)
        far = mm(c_out, entering[:, at].astype(BF16)) * mm(grow, spread[:, at])
        half = z[0, :, at].astype(F32) * 0.5
        value = (y[0, :, at].astype(F32) + far) * (half + half * jnp.tanh(half))
        kept = (value * gain[:, at]).astype(BF16)
        gated[0, :, at] = kept
        power = value * value
        for j in range(TILE // 128):
            square = square + power[:, j * 128 : (j + 1) * 128]
    wide = jnp.broadcast_to(jnp.sum(square, axis=1, keepdims=True), (CHUNK, 128))
    squares[pl.ds(row, 1), :] = wide.T[0:1, :]
    hi, mid, lo = three(wide)
    lane = lax.broadcasted_iota(jnp.int32, (CHUNK, EXTRA), 1)
    extra = jnp.where(lane == 0, hi, jnp.where(lane == 1, mid, jnp.where(lane == 2, lo, 0.0)))
    routed[:, pl.ds(0, feats)] += mm(pick, gated[0])
    routed[:, pl.ds(feats, EXTRA)] += mm(pick, extra.astype(BF16))

    @pl.when(row == pl.num_programs(0) * pl.num_programs(1) - 1)
    def _():
        for d in range(groups):
            sends[d][...] = routed[pl.ds(d * share, share), :].astype(BF16)


def gate(me, pieces, y, z, c, cum, gain, slot_pos, spread):
    count, length, feats = z.shape
    groups = len(pieces)
    slots = slot_pos.shape[0]
    fixed = lambda shape: pl.BlockSpec(shape, lambda s, i, m: (0,) * len(shape))
    block = lambda width: pl.BlockSpec((1, CHUNK, width), lambda s, i, m: (s, i, 0))
    send = (slots // groups, feats + EXTRA)
    lines = (count * length // CHUNK, 128)
    return pl.pallas_call(
        functools.partial(gate_kernel, groups, feats // HEAD_DIM, slots),
        grid_spec=pltpu.PrefetchScalarGridSpec(
            num_scalar_prefetch=1,
            grid=(count, length // CHUNK),
            in_specs=[fixed(pieces[0].shape)] * groups
            + [block(feats), block(feats), block(NSTATE), block(128)]
            + [fixed((1, feats)), fixed((slots, 1)), pl.BlockSpec(memory_space=pltpu.VMEM)],
            out_specs=[block(feats), fixed(lines)] + [fixed(send)] * groups,
            scratch_shapes=[
                pltpu.VMEM((NSTATE, feats), F32),
                pltpu.VMEM((slots, feats + EXTRA), F32),
            ],
        ),
        out_shape=[jax.ShapeDtypeStruct((count, length, feats), BF16), jax.ShapeDtypeStruct(lines, F32)]
        + [jax.ShapeDtypeStruct(send, BF16)] * groups,
        compiler_params=pltpu.CompilerParams(vmem_limit_bytes=60 << 20),
        cost_estimate=pl.CostEstimate(flops=2_000_000_000, bytes_accessed=20_000_000, transcendentals=0),
        name="gate",
    )(me, *pieces, y, z, c, cum, gain, slot_pos, spread)


def scale_kernel(gated, mine, other, *rest):
    out, token = rest[-2:]
    token[...] = jnp.zeros_like(token)
    row = pl.ds(pl.program_id(0) * pl.num_programs(1) + pl.program_id(1), 1)
    mean = (mine[row, :] + other[row, :]) / (HEAD_TOTAL * HEAD_DIM)
    inv = jnp.broadcast_to(lax.rsqrt(mean + norm_eps), (CHUNK, 128)).T
    for i in range(gated.shape[2] // 128):
        at = pl.ds(i * 128, 128)
        out[0, :, at] = (gated[0, :, at].astype(F32) * inv).astype(BF16)


def scale(gated, mine, other, after):
    count, length, feats = gated.shape
    fixed = lambda shape: pl.BlockSpec(shape, lambda s, i: (0,) * len(shape))
    block = pl.BlockSpec((1, CHUNK, feats), lambda s, i: (s, i, 0))
    return pl.pallas_call(
        scale_kernel,
        grid=(count, length // CHUNK),
        in_specs=[block, fixed(mine.shape), fixed(mine.shape)]
        + [pl.BlockSpec(memory_space=pl.ANY)] * len(after),
        out_specs=[block, fixed((8, 128))],
        out_shape=[jax.ShapeDtypeStruct(gated.shape, BF16), jax.ShapeDtypeStruct((8, 128), F32)],
        compiler_params=pltpu.CompilerParams(vmem_limit_bytes=10 << 20),
        cost_estimate=pl.CostEstimate(flops=10_000_000, bytes_accessed=8_000_000, transcendentals=0),
        name="scale",
    )(gated, mine, other, *after)


def join_kernel(count, *refs):
    out = refs[-1]
    share = refs[0].shape[0]
    for k in range(count):
        out[pl.ds(k * share, share), :] = refs[k][...]


def join(parts, after):
    share, wide = parts[0].shape
    vmem = pl.BlockSpec(memory_space=pltpu.VMEM)
    return pl.pallas_call(
        functools.partial(join_kernel, len(parts)),
        in_specs=[vmem] * len(parts) + [pl.BlockSpec(memory_space=pl.ANY)] * len(after),
        out_specs=vmem,
        out_shape=jax.ShapeDtypeStruct((len(parts) * share, wide), BF16),
        compiler_params=pltpu.CompilerParams(vmem_limit_bytes=10 << 20),
        cost_estimate=pl.CostEstimate(flops=1_000_000, bytes_accessed=700_000, transcendentals=0),
        name="join",
    )(*parts, *after)


def expert_kernel(core, own, other, w1, b1, w2, *outs):
    feats = own.shape[1] - EXTRA
    share = outs[0].shape[0]
    sums = jnp.zeros((own.shape[0], 1), F32)
    for ref in (own, other):
        part = ref[:, pl.ds(feats, EXTRA)].astype(F32)
        lane = lax.broadcasted_iota(jnp.int32, part.shape, 1)
        sums = sums + jnp.sum(jnp.where(lane < 3, part, 0.0), axis=1, keepdims=True)
    inv = lax.rsqrt(sums / (HEAD_TOTAL * HEAD_DIM) + norm_eps)
    lower = pl.ds(pl.multiple_of(core[0] * feats, 128), feats)
    upper = pl.ds(pl.multiple_of((1 - core[0]) * feats, 128), feats)
    pre = mm(own[:, pl.ds(0, feats)], w1[0, lower, :]) + mm(
        other[:, pl.ds(0, feats)], w1[0, upper, :]
    )
    pre = pre * inv + b1[...]
    hidden = jax.nn.gelu(pre).astype(BF16).astype(F32)
    value = jnp.sum(hidden * w2[...].astype(F32), axis=1, keepdims=True)
    value = jnp.broadcast_to(value, (own.shape[0], 128))
    for k, out in enumerate(outs):
        out[...] = value[k * share : (k + 1) * share]


def expert(core, own, other, w1, b1, w2, count):
    share = own.shape[0] // count
    vmem = pl.BlockSpec(memory_space=pltpu.VMEM)
    return pl.pallas_call(
        expert_kernel,
        in_specs=[pl.BlockSpec(memory_space=pltpu.SMEM)] + [vmem] * 5,
        out_specs=[vmem] * count,
        out_shape=[jax.ShapeDtypeStruct((share, 128), F32)] * count,
        compiler_params=pltpu.CompilerParams(vmem_limit_bytes=14 << 20),
        cost_estimate=pl.CostEstimate(flops=400_000_000, bytes_accessed=6_000_000, transcendentals=0),
        name="expert",
    )(core, own, other, w1, b1, w2)


def body(
    x_inner,
    z_gate,
    b_input,
    c_output,
    step_sizes,
    decay_log,
    skip_gain,
    norm_gain,
    goal_pos,
    goal_owner,
    value_w1,
    value_b1,
    value_w2,
):
    count, length, feats = x_inner.shape
    heads = step_sizes.shape[2]
    devices = lax.axis_size("seq")
    planes = PLANES
    groups = devices // planes
    index = lax.axis_index("seq")
    place, plane = index % groups, index // groups
    me = place.reshape(1).astype(jnp.int32)
    core = lax.axis_index("head").reshape(1).astype(jnp.int32)

    def permute(value, where):
        return lax.ppermute(value, "seq", where)

    def across(value, d):
        return permute(value, [(i, i ^ d) for i in range(devices)])

    def swap(value):
        return lax.ppermute(value, "head", [(0, 1), (1, 0)])

    def triple(v, fill):
        return jnp.concatenate(
            [v, v, v, jnp.full(v.shape[:-1] + (128 - 3 * heads,), fill, F32)], axis=-1
        )

    lanes = np.arange(128)
    spread = jnp.asarray(
        (lanes[:, None] % heads == np.arange(feats)[None, :] // HEAD_DIM)
        & (lanes[:, None] < 3 * heads),
        BF16,
    )
    dt = jnp.swapaxes(step_sizes, 1, 2)
    rate = triple(-jnp.exp(decay_log) * LOG2E, 0.0)[None]
    skip = triple(skip_gain, 0.0)[None]
    gain = norm_gain[None]

    goal_dev = goal_pos.shape[1]
    owners = goal_owner.reshape(-1)
    positions = (
        goal_pos - index * length + length * jnp.arange(count, dtype=jnp.int32)[:, None]
    ).reshape(-1)
    ids = jnp.arange(owners.shape[0])
    same = (owners[:, None] == owners[None, :]) & (ids[None, :] < ids[:, None])
    rank = jnp.sum(same.astype(jnp.int32), axis=1)
    slot = (((owners % groups) ^ place) * planes + ((owners // groups) ^ plane)) * CAP + rank
    slots = devices * CAP
    taken = jnp.arange(slots)[:, None] == slot[None, :]
    slot_pos = jnp.max(jnp.where(taken, positions[None, :], -1), axis=1, keepdims=True)

    nothing = jnp.zeros((1,), jnp.int32)

    def upward(value, hops):
        hop = hops * groups
        return permute(value, [(i, i + hop) for i in range(devices - hop)])

    def local(s, part, parts, before, after):
        return local_part(
            s, part, parts, x_inner, b_input, c_output, dt, rate, skip, spread, before, after
        )

    def spread_out(own):
        return [own[0]] + [across(own[d], d) for d in range(1, groups)]

    *own, cum = summary(me, x_inner, b_input, dt, rate, spread, groups)
    gathered = spread_out(own)
    y, token = local(0, 0, 1, (), (own[0],))
    total = plane_total(me, spread, gathered, count, (token,))
    one = upward(total, 1)
    y, token = local(1, 0, 2, (y,), (total,))
    pair = plane_total(nothing, spread, [one, total], count, (token,))
    two = upward(pair, 2)
    y, token = local(1, 1, 2, (y,), (pair,))
    entering = spread_out(incoming_states(me, spread, gathered, [one, two], count, (token,)))
    gated, mine, *sends = gate(
        me, entering, y, z_gate, c_output, cum, gain, slot_pos, spread
    )
    near = spread_out(sends)
    far = [
        jnp.concatenate([v[k * CAP : (k + 1) * CAP] for v in near], axis=0) for k in range(planes)
    ]
    own = [far[0]] + [across(far[k], k * groups) for k in range(1, planes)]
    layer_out, token = scale(gated, mine, swap(mine), (far[1],))
    rows = join(own, (token,))
    answers = expert(core, rows, swap(rows), value_w1, value_b1, value_w2, planes)
    answers = [v[:, :1] for v in answers]
    back = [answers[0]] + [across(answers[k], k * groups) for k in range(1, planes)]
    table = jnp.concatenate(back, axis=1)
    table = table + swap(table)
    tables = [table] + [across(table, d) for d in range(1, groups)]
    flat = jnp.concatenate(
        [t[d * CAP : (d + 1) * CAP].T.reshape(-1) for d, t in enumerate(tables)]
    )
    values = jnp.sum(jnp.where(taken, flat[:, None], 0.0), axis=0).reshape(count, goal_dev)
    return (layer_out, values)


def solution(mesh):
    placed = (
        P(None, "seq", "head"),
        P(None, "seq", "head"),
        P(None, "seq", None),
        P(None, "seq", None),
        P(None, "seq", "head"),
        P("head"),
        P("head"),
        P("head"),
        P(None, "seq"),
        P(None, "seq"),
        P("seq", None, "head"),
        P("seq", "head"),
        P("seq", "head"),
    )
    return jax.shard_map(
        body,
        mesh=mesh,
        in_specs=placed,
        out_specs=(P(None, "seq", "head"), P(None, "seq")),
        check_vma=False,
    )
```

time: 162 us -> 145 us (0.90)
  local copies, waits for them, and re-layouts: 34.3 us -> 14.2 us
  starting transfers between devices: 56.2 us -> 37.4 us
  Pallas kernels: 46.3 us -> 60.8 us
  waiting for transfers between devices: 20.4 us -> 27.5 us
    unnamed x51 -> x44, local copies, waits for them, and re-layouts: 32.3 us -> 10.3 us
    ppermute x30 -> x20, starting transfers between devices: 54.9 us -> 37.2 us  [permute(): return lax.ppermute(value, 'seq', where)]
    pallas_call x9, Pallas kernels: 34.4 us -> 47.5 us  [the longest x3 28.3 us: local_part(): pl.pallas_call(functools.partial(local_kernel, heads, part * feats // HEA...]
    ppermute x30 -> x20, waiting for transfers between devices: 19.3 us -> 24.7 us  [permute(): return lax.ppermute(value, 'seq', where)]
    pallas_call x2 -> x1, Pallas kernels: 9.53 us -> 12.5 us  [summary(): pl.pallas_call(functools.partial(summary_kernel, groups, heads), grid_spe...]
    pallas_call x2 -> x1, Pallas kernels: 2.43 us -> 0.77 us  [incoming_states(): pl.pallas_call(functools.partial(incoming_kernel, groups, hops, feats //...]
  transfers between devices with their start and end apart: 37 -> 23, of which waited for: 12 -> 12; matrix products, arithmetic and copies ran while one was open for 1% -> 3% of each run, Pallas kernels for 23% -> 23%
where the time goes in v2:
time: 145 us; the launch traced here: 144 us
  Pallas kernels  60.8 us (42%)
  starting transfers between devices  37.4 us (26%)
  waiting for transfers between devices  27.5 us (19%)
  local copies, waits for them, and re-layouts  14.2 us (10%)
  other arithmetic  2.91 us (2%)
    ppermute x20, starting transfers between devices, permute(): return lax.ppermute(value, 'seq', where)  37.2 us
    pallas_call x3, Pallas kernels, local_part(): pl.pallas_call(functools.partial(local_kernel, heads, part * feats // HEA...  28.3 us
    ppermute x20, waiting for transfers between devices, permute(): return lax.ppermute(value, 'seq', where)  24.7 us
    pallas_call x1, Pallas kernels, gate(): pl.pallas_call(functools.partial(gate_kernel, groups, feats // HEAD_DIM,...  12.8 us
    pallas_call x1, Pallas kernels, summary(): pl.pallas_call(functools.partial(summary_kernel, groups, heads), grid_spe...  12.5 us
    unnamed x44, local copies, waits for them, and re-layouts  10.3 us
    pallas_call x1, Pallas kernels, scale(): pl.pallas_call(scale_kernel, grid=(count, length // CHUNK), in_specs=[blo...  4.39 us
  transfers between devices with their start and end apart: 23, of which 12 were waited for; matrix products, arithmetic and copies ran while one was open for 3% of the time, Pallas kernels for 23%

profile of v2, /device:TPU:0, one launch (start us, length us, event | category | flops | bytes accessed | tf_op | source)
XLA Modules:
  0.0 143.8 jit_solution(14600454289618741388)
XLA Ops:
  1.3 1.4 %fusion.2 = (f32[1,128]{1,0:T(1,128)}, f32[1,128]{1,0:T(1,128)}) fusion(f32[8]{0:T(128)S(1)} %broadcast.86, f32[40]{0:T(128)} %param.20, f32[40]{0:T(128)S(1)} %negate_multiply_fusion), kind=kLoop, calls=%fused_computation.24 | loop fusion | flops 768 | bytes 1376 | tf_op jit(solution)/shard_map/broadcast_in_dim | solution.py:552
  2.8 12.5 %summary.1 = (bf16[64,2688]{1,0:T(8,128)(2,1)}, bf16[64,2688]{1,0:T(8,128)(2,1)}, bf16[64,2688]{1,0:T(8,128)(2,1)}, bf16[64,2688]{1,0:T(8,128)(2,1)}, f32[2,512,128]{2,1,0:T(8,128)}) custom-call(s32[1]{0:T(128)} %bitcast.me, bf16[2,512,2560]{2,1,0:T(8,128)(2,1)} %x.7, bf16[2,512,128]{2,1,0:T(8,128)(2,1)} %b.7, f32[2,40,512]{2,1,0:T(8,128)} %bitcast.25, ...), custom_call_target="tpu_custom_call" | custom-call | flops 2800000000 | bytes 8000000 | tf_op jit(solution)/shard_map/summary/pallas_call | solution.py:112
  15.3 2.9 %collective-permute-start = (bf16[64,2688]{1,0:T(8,128)(2,1)}, bf16[64,2688]{1,0:T(8,128)(2,1)S(1)}, u32[]{:S(2)}, u32[]{:S(2)}) collective-permute-start(bf16[64,2688]{1,0:T(8,128)(2,1)} %get-tuple-element.30), channel_id=1, source_target_pairs={{0,2},{2,0},{4,6},{6,4},{8,10},{10,8},{12,14},{14,12},{16,18},{18,... | collective-permute-start | bytes 1032200 | tf_op jit(solution)/shard_map/ppermute | solution.py:531
  18.2 1.5 %collective-permute-start.1 = (bf16[64,2688]{1,0:T(8,128)(2,1)}, bf16[64,2688]{1,0:T(8,128)(2,1)S(1)}, u32[]{:S(2)}, u32[]{:S(2)}) collective-permute-start(bf16[64,2688]{1,0:T(8,128)(2,1)} %get-tuple-element.31), channel_id=1, source_target_pairs={{0,4},{2,6},{4,0},{6,2},{8,12},{10,14},{12,8},{14,10},{16,20},{18,... | collective-permute-start | bytes 1032200 | tf_op jit(solution)/shard_map/ppermute | solution.py:531
  20.2 12.4 %local_part.3 = (bf16[2,512,2560]{2,1,0:T(8,128)(2,1)}, f32[8,128]{1,0:T(8,128)}) custom-call(bf16[2,512,2560]{2,1,0:T(8,128)(2,1)} %x.7, bf16[2,512,128]{2,1,0:T(8,128)(2,1)} %b.7, bf16[2,512,128]{2,1,0:T(8,128)(2,1)} %refs_6_.1, f32[2,40,512]{2,1,0:T(8,128)} %bitcast.26, f32[1,128]{1,0:T(1,128)} %get-tuple-element.73.rate, ...), custom_call_target="tpu_custom_call" | custom-call | flops 6000000000 | bytes 9000000 | tf_op jit(solution)/shard_map/local_part/pallas_call | solution.py:308
  32.6 2.7 %collective-permute-done.1.rest_2_ = bf16[64,2688]{1,0:T(8,128)(2,1)S(1)} collective-permute-done((bf16[64,2688]{1,0:T(8,128)(2,1)}, bf16[64,2688]{1,0:T(8,128)(2,1)S(1)}, u32[]{:S(2)}, u32[]{:S(2)}) %collective-permute-start.1) | collective-permute-done | bytes 344096 | tf_op jit(solution)/shard_map/ppermute | solution.py:531
  36.5 3.5 %collective-permute-start.3 = (bf16[64,2688]{1,0:T(8,128)(2,1)S(1)}, bf16[64,2688]{1,0:T(8,128)(2,1)S(1)}, u32[]{:S(2)}, u32[]{:S(2)}) collective-permute-start(bf16[64,2688]{1,0:T(8,128)(2,1)S(1)} %plane_total.2.rest_1_), channel_id=1, source_target_pairs={{0,8},{2,10},{4,12},{6,14},{8,16},{10,18},{12,20},{14,22},{16,24},... | collective-permute-start | bytes 1032200 | tf_op jit(solution)/shard_map/ppermute | solution.py:531
  40.1 8.0 %local_part.4 = (bf16[2,512,2560]{2,1,0:T(8,128)(2,1)}, f32[8,128]{1,0:T(8,128)}) custom-call(bf16[2,512,2560]{2,1,0:T(8,128)(2,1)} %x.7, bf16[2,512,128]{2,1,0:T(8,128)(2,1)} %b.7, bf16[2,512,128]{2,1,0:T(8,128)(2,1)} %refs_6_.1, f32[2,40,512]{2,1,0:T(8,128)} %bitcast.27, f32[1,128]{1,0:T(1,128)} %get-tuple-element.73.rate, ...), custom_call_target="tpu_custom_call", output_to_operand_aliasing={{0}: (7, {})} | custom-call | flops 6000000000 | bytes 9000000 | tf_op jit(solution)/shard_map/local_part/pallas_call | solution.py:308
  50.1 4.7 %collective-permute-start.4 = (bf16[64,2688]{1,0:T(8,128)(2,1)S(1)}, bf16[64,2688]{1,0:T(8,128)(2,1)S(1)}, u32[]{:S(2)}, u32[]{:S(2)}) collective-permute-start(bf16[64,2688]{1,0:T(8,128)(2,1)S(1)} %plane_total.3.rest_1_), channel_id=1, source_target_pairs={{0,16},{2,18},{4,20},{6,22},{8,24},{10,26},{12,28},{14,30},{1,17},... | collective-permute-start | bytes 1032200 | tf_op jit(solution)/shard_map/ppermute | solution.py:531
  54.8 7.9 %local_part.5 = (bf16[2,512,2560]{2,1,0:T(8,128)(2,1)}, f32[8,128]{1,0:T(8,128)}) custom-call(bf16[2,512,2560]{2,1,0:T(8,128)(2,1)} %x.7, bf16[2,512,128]{2,1,0:T(8,128)(2,1)} %b.7, bf16[2,512,128]{2,1,0:T(8,128)(2,1)} %refs_6_.1, f32[2,40,512]{2,1,0:T(8,128)} %bitcast.28, f32[1,128]{1,0:T(1,128)} %get-tuple-element.73.rate, ...), custom_call_target="tpu_custom_call", output_to_operand_aliasing={{0}: (7, {})} | custom-call | flops 6000000000 | bytes 9000000 | tf_op jit(solution)/shard_map/local_part/pallas_call | solution.py:308
  65.0 1.2 collective-permute-start.5
  67.0 1.4 collective-permute-start.7
  69.9 5.7 %collective-permute-done.5.refs_1_ = bf16[64,2560]{1,0:T(8,128)(2,1)S(1)} collective-permute-done((bf16[64,2560]{1,0:T(8,128)(2,1)S(1)}, bf16[64,2560]{1,0:T(8,128)(2,1)S(1)}, u32[]{:S(2)}, u32[]{:S(2)}) %collective-permute-start.5) | collective-permute-done | bytes 327712 | tf_op jit(solution)/shard_map/ppermute | solution.py:531
  75.6 5.3 %collective-permute-done.6.refs_2_ = bf16[64,2560]{1,0:T(8,128)(2,1)S(1)} collective-permute-done((bf16[64,2560]{1,0:T(8,128)(2,1)S(1)}, bf16[64,2560]{1,0:T(8,128)(2,1)S(1)}, u32[]{:S(2)}, u32[]{:S(2)}) %collective-permute-start.6) | collective-permute-done | bytes 327712 | tf_op jit(solution)/shard_map/ppermute | solution.py:531
  81.8 12.8 %gate.1 = (bf16[2,512,2560]{2,1,0:T(8,128)(2,1)}, f32[8,128]{1,0:T(8,128)}, bf16[16,2688]{1,0:T(8,128)(2,1)}, bf16[16,2688]{1,0:T(8,128)(2,1)}, bf16[16,2688]{1,0:T(8,128)(2,1)}, /*index=5*/bf16[16,2688]{1,0:T(8,128)(2,1)}) custom-call(s32[1]{0:T(128)} %bitcast.me, bf16[64,2560]{1,0:T(8,128)(2,1)} %copy-done.9, bf16[64,2560]{1,0:T(8,128)(2,1)} %copy-done.16, ...), custom_call_target="tpu_custom_call" | custom-call | flops 2000000000 | bytes 20000000 | tf_op jit(solution)/shard_map/gate/pallas_call | solution.py:398
  95.3 1.0 collective-permute-start.10
  96.3 1.9 %collective-permute-start.11 = (bf16[16,2688]{1,0:T(8,128)(2,1)}, bf16[16,2688]{1,0:T(8,128)(2,1)S(1)}, u32[]{:S(2)}, u32[]{:S(2)}) collective-permute-start(bf16[16,2688]{1,0:T(8,128)(2,1)} %get-tuple-element.49), channel_id=1, source_target_pairs={{0,6},{2,4},{4,2},{6,0},{8,14},{10,12},{12,10},{14,8},{16,22},{18,... | collective-permute-start | bytes 258056 | tf_op jit(solution)/shard_map/ppermute | solution.py:531
  100.0 1.9 %collective-permute-done.11 = bf16[16,2688]{1,0:T(8,128)(2,1)S(1)} collective-permute-done((bf16[16,2688]{1,0:T(8,128)(2,1)}, bf16[16,2688]{1,0:T(8,128)(2,1)S(1)}, u32[]{:S(2)}, u32[]{:S(2)}) %collective-permute-start.11) | collective-permute-done | bytes 86048 | tf_op jit(solution)/shard_map/ppermute | solution.py:531
  102.0 8.9 %collective-permute-start.14 = (bf16[16,2688]{1,0:T(8,128)(2,1)S(1)}, bf16[16,2688]{1,0:T(8,128)(2,1)S(1)}, u32[]{:S(2)}, u32[]{:S(2)}) collective-permute-start(bf16[16,2688]{1,0:T(8,128)(2,1)S(1)} %pad_maximum_fusion.3), channel_id=1, source_target_pairs={{0,24},{2,26},{4,28},{6,30},{8,16},{10,18},{12,20},{14,22},{16,8},... | collective-permute-start | bytes 258056 | tf_op jit(solution)/shard_map/ppermute | solution.py:531
  111.8 2.5 %copy-done.4 = bf16[2,512,2560]{2,1,0:T(8,128)(2,1)S(1)} copy-done((bf16[2,512,2560]{2,1,0:T(8,128)(2,1)S(1)}, bf16[2,512,2560]{2,1,0:T(8,128)(2,1)}, u32[]{:S(2)}) %copy-start.4) | copy-done | bytes 5242904
  114.9 4.4 %scale.1 = (bf16[2,512,2560]{2,1,0:T(8,128)(2,1)}, f32[8,128]{1,0:T(8,128)S(1)}) custom-call(bf16[2,512,2560]{2,1,0:T(8,128)(2,1)S(1)} %copy-done.4, f32[8,128]{1,0:T(8,128)S(1)} %copy-done.10, f32[8,128]{1,0:T(8,128)S(1)} %collective-permute-done.8.other, bf16[16,2688]{1,0:T(8,128)(2,1)S(1)} %pad_maximum_fusion.rest_0_), custom_call_target="tpu_custom_call" | custom-call | flops 10000000 | bytes 8000000 | tf_op jit(solution)/shard_map/scale/pallas_call | solution.py:435
  119.5 1.6 %collective-permute-done.15.other = bf16[64,2688]{1,0:T(8,128)(2,1)S(1)} collective-permute-done((bf16[64,2688]{1,0:T(8,128)(2,1)S(1)}, bf16[64,2688]{1,0:T(8,128)(2,1)S(1)}, u32[]{:S(2)}, u32[]{:S(2)}) %collective-permute-start.15) | collective-permute-done | bytes 344096 | tf_op jit(solution)/shard_map/ppermute | solution.py:537
  121.1 2.5 %copy-done.3 = bf16[1,5120,512]{2,1,0:T(8,128)(2,1)S(1)} copy-done((bf16[1,5120,512]{2,1,0:T(8,128)(2,1)S(1)}, bf16[1,5120,512]{2,1,0:T(8,128)(2,1)}, u32[]{:S(2)}) %copy-start.3) | copy-done | bytes 5242904
  123.6 1.1 expert.1
  124.7 1.5 %collective-permute-start.16 = (f32[16,1]{1,0:T(8,128)S(1)}, f32[16,1]{1,0:T(8,128)S(1)}, u32[]{:S(2)}, u32[]{:S(2)}) collective-permute-start(f32[16,1]{1,0:T(8,128)S(1)} %bitcast.23), channel_id=1, source_target_pairs={{0,8},{2,10},{4,12},{6,14},{8,0},{10,2},{12,4},{14,6},{16,24},{18,... | collective-permute-start | bytes 200 | tf_op jit(solution)/shard_map/ppermute | solution.py:531
  126.2 2.9 %collective-permute-start.17 = (f32[16,1]{1,0:T(8,128)S(1)}, f32[16,1]{1,0:T(8,128)S(1)}, u32[]{:S(2)}, u32[]{:S(2)}) collective-permute-start(f32[16,1]{1,0:T(8,128)S(1)} %bitcast.22), channel_id=1, source_target_pairs={{0,16},{2,18},{4,20},{6,22},{8,24},{10,26},{12,28},{14,30},{16,0},... | collective-permute-start | bytes 200 | tf_op jit(solution)/shard_map/ppermute | solution.py:531
  129.3 1.5 %collective-permute-done.17 = f32[16,1]{1,0:T(8,128)S(1)} collective-permute-done((f32[16,1]{1,0:T(8,128)S(1)}, f32[16,1]{1,0:T(8,128)S(1)}, u32[]{:S(2)}, u32[]{:S(2)}) %collective-permute-start.17) | collective-permute-done | bytes 96 | tf_op jit(solution)/shard_map/ppermute | solution.py:531
  130.8 3.7 %collective-permute-done.18 = f32[16,1]{1,0:T(8,128)S(1)} collective-permute-done((f32[16,1]{1,0:T(8,128)S(1)}, f32[16,1]{1,0:T(8,128)S(1)}, u32[]{:S(2)}, u32[]{:S(2)}) %collective-permute-start.18) | collective-permute-done | bytes 96 | tf_op jit(solution)/shard_map/ppermute | solution.py:531
  134.7 1.1 collective-permute-done.19
  136.6 1.7 %collective-permute-start.21 = (f32[16,4]{0,1:T(4,128)S(1)}, f32[16,4]{0,1:T(4,128)S(1)}, u32[]{:S(2)}, u32[]{:S(2)}) collective-permute-start(f32[16,4]{0,1:T(4,128)S(1)} %fusion.6), channel_id=1, source_target_pairs={{0,4},{2,6},{4,0},{6,2},{8,12},{10,14},{12,8},{14,10},{16,20},{18,... | collective-permute-start | bytes 776 | tf_op jit(solution)/shard_map/ppermute | solution.py:531
  138.4 1.1 collective-permute-start.22
  140.5 2.4 %collective-permute-done.22 = f32[16,4]{0,1:T(4,128)S(1)} collective-permute-done((f32[16,4]{0,1:T(4,128)S(1)}, f32[16,4]{0,1:T(4,128)S(1)}, u32[]{:S(2)}, u32[]{:S(2)}) %collective-permute-start.22) | collective-permute-done | bytes 288 | tf_op jit(solution)/shard_map/ppermute | solution.py:531
  (106 shorter events, 17.0 us)
Async XLA Ops:
  0.6 19.1 %copy-start.21 = (s32[2,32]{1,0:T(2,128)S(1)}, s32[2,32]{1,0:T(2,128)}, u32[]{:S(2)}) copy-start(s32[2,32]{1,0:T(2,128)} %param.23) | copy-start | bytes 772
  0.6 19.4 %copy-start.20 = (s32[2,32]{1,0:T(2,128)S(1)}, s32[2,32]{1,0:T(2,128)}, u32[]{:S(2)}) copy-start(s32[2,32]{1,0:T(2,128)} %param.22) | copy-start | bytes 772
  15.3 17.3 %collective-permute-start = (bf16[64,2688]{1,0:T(8,128)(2,1)}, bf16[64,2688]{1,0:T(8,128)(2,1)S(1)}, u32[]{:S(2)}, u32[]{:S(2)}) collective-permute-start(bf16[64,2688]{1,0:T(8,128)(2,1)} %get-tuple-element.30), channel_id=1, source_target_pairs={{0,2},{2,0},{4,6},{6,4},{8,10},{10,8},{12,14},{14,12},{16,18},{18,... | collective-permute-start | bytes 1032200 | tf_op jit(solution)/shard_map/ppermute | solution.py:531
  18.2 17.1 %collective-permute-start.1 = (bf16[64,2688]{1,0:T(8,128)(2,1)}, bf16[64,2688]{1,0:T(8,128)(2,1)S(1)}, u32[]{:S(2)}, u32[]{:S(2)}) collective-permute-start(bf16[64,2688]{1,0:T(8,128)(2,1)} %get-tuple-element.31), channel_id=1, source_target_pairs={{0,4},{2,6},{4,0},{6,2},{8,12},{10,14},{12,8},{14,10},{16,20},{18,... | collective-permute-start | bytes 1032200 | tf_op jit(solution)/shard_map/ppermute | solution.py:531
  19.7 15.6 %collective-permute-start.2 = (bf16[64,2688]{1,0:T(8,128)(2,1)}, bf16[64,2688]{1,0:T(8,128)(2,1)S(1)}, u32[]{:S(2)}, u32[]{:S(2)}) collective-permute-start(bf16[64,2688]{1,0:T(8,128)(2,1)} %get-tuple-element.32), channel_id=1, source_target_pairs={{0,6},{2,4},{4,2},{6,0},{8,14},{10,12},{12,10},{14,8},{16,22},{18,... | collective-permute-start | bytes 1032200 | tf_op jit(solution)/shard_map/ppermute | solution.py:531
  20.2 15.1 %copy-start = (bf16[128,2560]{1,0:T(8,128)(2,1)S(1)}, bf16[128,2560]{1,0:T(8,128)(2,1)}, u32[]{:S(2)}) copy-start(bf16[128,2560]{1,0:T(8,128)(2,1)} %constant.68.clone.spread.refs_10_) | copy-start | bytes 1966084
  20.2 15.1 %copy-start.5 = (bf16[64,2688]{1,0:T(8,128)(2,1)S(1)}, bf16[64,2688]{1,0:T(8,128)(2,1)}, u32[]{:S(2)}) copy-start(bf16[64,2688]{1,0:T(8,128)(2,1)} %get-tuple-element.29.rest_0_) | copy-start | bytes 1032196
  36.5 11.5 %collective-permute-start.3 = (bf16[64,2688]{1,0:T(8,128)(2,1)S(1)}, bf16[64,2688]{1,0:T(8,128)(2,1)S(1)}, u32[]{:S(2)}, u32[]{:S(2)}) collective-permute-start(bf16[64,2688]{1,0:T(8,128)(2,1)S(1)} %plane_total.2.rest_1_), channel_id=1, source_target_pairs={{0,8},{2,10},{4,12},{6,14},{8,16},{10,18},{12,20},{14,22},{16,24},... | collective-permute-start | bytes 1032200 | tf_op jit(solution)/shard_map/ppermute | solution.py:531
  40.0 8.0 %copy-start.1 = (bf16[128,2560]{1,0:T(8,128)(2,1)S(1)}, bf16[128,2560]{1,0:T(8,128)(2,1)}, u32[]{:S(2)}) copy-start(bf16[128,2560]{1,0:T(8,128)(2,1)} %constant.68.clone.spread.refs_10_) | copy-start | bytes 1966084
  50.1 12.7 %collective-permute-start.4 = (bf16[64,2688]{1,0:T(8,128)(2,1)S(1)}, bf16[64,2688]{1,0:T(8,128)(2,1)S(1)}, u32[]{:S(2)}, u32[]{:S(2)}) collective-permute-start(bf16[64,2688]{1,0:T(8,128)(2,1)S(1)} %plane_total.3.rest_1_), channel_id=1, source_target_pairs={{0,16},{2,18},{4,20},{6,22},{8,24},{10,26},{12,28},{14,30},{1,17},... | collective-permute-start | bytes 1032200 | tf_op jit(solution)/shard_map/ppermute | solution.py:531
  54.8 8.0 %copy-start.2 = (bf16[128,2560]{1,0:T(8,128)(2,1)S(1)}, bf16[128,2560]{1,0:T(8,128)(2,1)}, u32[]{:S(2)}) copy-start(bf16[128,2560]{1,0:T(8,128)(2,1)} %constant.68.clone.spread.refs_10_) | copy-start | bytes 1966084
  54.8 14.5 %copy-start.19 = (f32[2560]{0:T(1024)S(1)}, f32[2560]{0:T(1024)}, u32[]{:S(2)}) copy-start(f32[2560]{0:T(1024)} %param.21) | copy-start | bytes 30724
  65.0 10.7 %collective-permute-start.5 = (bf16[64,2560]{1,0:T(8,128)(2,1)S(1)}, bf16[64,2560]{1,0:T(8,128)(2,1)S(1)}, u32[]{:S(2)}, u32[]{:S(2)}) collective-permute-start(bf16[64,2560]{1,0:T(8,128)(2,1)S(1)} %get-tuple-element.39), channel_id=1, source_target_pairs={{0,2},{2,0},{4,6},{6,4},{8,10},{10,8},{12,14},{14,12},{16,18},{18,... | collective-permute-start | bytes 983048 | tf_op jit(solution)/shard_map/ppermute | solution.py:531
  66.2 14.8 %collective-permute-start.6 = (bf16[64,2560]{1,0:T(8,128)(2,1)S(1)}, bf16[64,2560]{1,0:T(8,128)(2,1)S(1)}, u32[]{:S(2)}, u32[]{:S(2)}) collective-permute-start(bf16[64,2560]{1,0:T(8,128)(2,1)S(1)} %get-tuple-element.40), channel_id=1, source_target_pairs={{0,4},{2,6},{4,0},{6,2},{8,12},{10,14},{12,8},{14,10},{16,20},{18,... | collective-permute-start | bytes 983048 | tf_op jit(solution)/shard_map/ppermute | solution.py:531
  67.0 13.9 %collective-permute-start.7 = (bf16[64,2560]{1,0:T(8,128)(2,1)S(1)}, bf16[64,2560]{1,0:T(8,128)(2,1)S(1)}, u32[]{:S(2)}, u32[]{:S(2)}) collective-permute-start(bf16[64,2560]{1,0:T(8,128)(2,1)S(1)} %get-tuple-element.41), channel_id=1, source_target_pairs={{0,6},{2,4},{4,2},{6,0},{8,14},{10,12},{12,10},{14,8},{16,22},{18,... | collective-permute-start | bytes 983048 | tf_op jit(solution)/shard_map/ppermute | solution.py:531
  94.6 26.5 %copy-start.14 = (f32[1,512]{1,0:T(1,128)S(1)}, f32[1,512]{1,0:T(1,128)}, u32[]{:S(2)}) copy-start(f32[1,512]{1,0:T(1,128)} %b1.1) | copy-start | bytes 6148
  94.6 26.5 %copy-start.15 = (bf16[1,512]{1,0:T(2,128)(2,1)S(1)}, bf16[1,512]{1,0:T(2,128)(2,1)}, u32[]{:S(2)}) copy-start(bf16[1,512]{1,0:T(2,128)(2,1)} %w2.1) | copy-start | bytes 3076
  94.6 4.8 %collective-permute-start.9 = (bf16[16,2688]{1,0:T(8,128)(2,1)}, bf16[16,2688]{1,0:T(8,128)(2,1)S(1)}, u32[]{:S(2)}, u32[]{:S(2)}) collective-permute-start(bf16[16,2688]{1,0:T(8,128)(2,1)} %get-tuple-element.47), channel_id=1, source_target_pairs={{0,2},{2,0},{4,6},{6,4},{8,10},{10,8},{12,14},{14,12},{16,18},{18,... | collective-permute-start | bytes 258056 | tf_op jit(solution)/shard_map/ppermute | solution.py:531
  95.3 4.7 %collective-permute-start.10 = (bf16[16,2688]{1,0:T(8,128)(2,1)}, bf16[16,2688]{1,0:T(8,128)(2,1)S(1)}, u32[]{:S(2)}, u32[]{:S(2)}) collective-permute-start(bf16[16,2688]{1,0:T(8,128)(2,1)} %get-tuple-element.48), channel_id=1, source_target_pairs={{0,4},{2,6},{4,0},{6,2},{8,12},{10,14},{12,8},{14,10},{16,20},{18,... | collective-permute-start | bytes 258056 | tf_op jit(solution)/shard_map/ppermute | solution.py:531
  96.3 5.6 %collective-permute-start.11 = (bf16[16,2688]{1,0:T(8,128)(2,1)}, bf16[16,2688]{1,0:T(8,128)(2,1)S(1)}, u32[]{:S(2)}, u32[]{:S(2)}) collective-permute-start(bf16[16,2688]{1,0:T(8,128)(2,1)} %get-tuple-element.49), channel_id=1, source_target_pairs={{0,6},{2,4},{4,2},{6,0},{8,14},{10,12},{12,10},{14,8},{16,22},{18,... | collective-permute-start | bytes 258056 | tf_op jit(solution)/shard_map/ppermute | solution.py:531
  99.1 12.7 %collective-permute-start.8 = (f32[8,128]{1,0:T(8,128)}, f32[8,128]{1,0:T(8,128)S(1)}, u32[]{:S(2)}, u32[]{:S(2)}) collective-permute-start(f32[8,128]{1,0:T(8,128)} %get-tuple-element.45.mine), channel_id=1, source_target_pairs={{0,1},{1,0},{2,3},{3,2},{4,5},{5,4},{6,7},{7,6},{8,9},{9,8},{10,11... | collective-permute-start | bytes 12296 | tf_op jit(solution)/shard_map/ppermute | solution.py:537
  102.0 17.3 %collective-permute-start.14 = (bf16[16,2688]{1,0:T(8,128)(2,1)S(1)}, bf16[16,2688]{1,0:T(8,128)(2,1)S(1)}, u32[]{:S(2)}, u32[]{:S(2)}) collective-permute-start(bf16[16,2688]{1,0:T(8,128)(2,1)S(1)} %pad_maximum_fusion.3), channel_id=1, source_target_pairs={{0,24},{2,26},{4,28},{6,30},{8,16},{10,18},{12,20},{14,22},{16,8},... | collective-permute-start | bytes 258056 | tf_op jit(solution)/shard_map/ppermute | solution.py:531
  110.9 8.4 %collective-permute-start.13 = (bf16[16,2688]{1,0:T(8,128)(2,1)S(1)}, bf16[16,2688]{1,0:T(8,128)(2,1)S(1)}, u32[]{:S(2)}, u32[]{:S(2)}) collective-permute-start(bf16[16,2688]{1,0:T(8,128)(2,1)S(1)} %pad_maximum_fusion.2), channel_id=1, source_target_pairs={{0,16},{2,18},{4,20},{6,22},{8,24},{10,26},{12,28},{14,30},{16,0},... | collective-permute-start | bytes 258056 | tf_op jit(solution)/shard_map/ppermute | solution.py:531
  111.1 8.3 %collective-permute-start.12 = (bf16[16,2688]{1,0:T(8,128)(2,1)S(1)}, bf16[16,2688]{1,0:T(8,128)(2,1)S(1)}, u32[]{:S(2)}, u32[]{:S(2)}) collective-permute-start(bf16[16,2688]{1,0:T(8,128)(2,1)S(1)} %pad_maximum_fusion.rest_0_), channel_id=1, source_target_pairs={{0,8},{2,10},{4,12},{6,14},{8,0},{10,2},{12,4},{14,6},{16,24},{18,... | collective-permute-start | bytes 258056 | tf_op jit(solution)/shard_map/ppermute | solution.py:531
  119.4 1.7 %collective-permute-start.15 = (bf16[64,2688]{1,0:T(8,128)(2,1)S(1)}, bf16[64,2688]{1,0:T(8,128)(2,1)S(1)}, u32[]{:S(2)}, u32[]{:S(2)}) collective-permute-start(bf16[64,2688]{1,0:T(8,128)(2,1)S(1)} %join.1.own), channel_id=1, source_target_pairs={{0,1},{1,0},{2,3},{3,2},{4,5},{5,4},{6,7},{7,6},{8,9},{9,8},{10,11... | collective-permute-start | bytes 1032200 | tf_op jit(solution)/shard_map/ppermute | solution.py:537
  124.7 4.5 %collective-permute-start.16 = (f32[16,1]{1,0:T(8,128)S(1)}, f32[16,1]{1,0:T(8,128)S(1)}, u32[]{:S(2)}, u32[]{:S(2)}) collective-permute-start(f32[16,1]{1,0:T(8,128)S(1)} %bitcast.23), channel_id=1, source_target_pairs={{0,8},{2,10},{4,12},{6,14},{8,0},{10,2},{12,4},{14,6},{16,24},{18,... | collective-permute-start | bytes 200 | tf_op jit(solution)/shard_map/ppermute | solution.py:531
  126.2 4.6 %collective-permute-start.17 = (f32[16,1]{1,0:T(8,128)S(1)}, f32[16,1]{1,0:T(8,128)S(1)}, u32[]{:S(2)}, u32[]{:S(2)}) collective-permute-start(f32[16,1]{1,0:T(8,128)S(1)} %bitcast.22), channel_id=1, source_target_pairs={{0,16},{2,18},{4,20},{6,22},{8,24},{10,26},{12,28},{14,30},{16,0},... | collective-permute-start | bytes 200 | tf_op jit(solution)/shard_map/ppermute | solution.py:531
  129.1 5.4 %collective-permute-start.18 = (f32[16,1]{1,0:T(8,128)S(1)}, f32[16,1]{1,0:T(8,128)S(1)}, u32[]{:S(2)}, u32[]{:S(2)}) collective-permute-start(f32[16,1]{1,0:T(8,128)S(1)} %bitcast.21), channel_id=1, source_target_pairs={{0,24},{2,26},{4,28},{6,30},{8,16},{10,18},{12,20},{14,22},{16,8},... | collective-permute-start | bytes 200 | tf_op jit(solution)/shard_map/ppermute | solution.py:531
  134.6 1.2 collective-permute-start.19
  135.9 3.7 %collective-permute-start.20 = (f32[16,4]{0,1:T(4,128)S(1)}, f32[16,4]{0,1:T(4,128)S(1)}, u32[]{:S(2)}, u32[]{:S(2)}) collective-permute-start(f32[16,4]{0,1:T(4,128)S(1)} %fusion.6), channel_id=1, source_target_pairs={{0,2},{2,0},{4,6},{6,4},{8,10},{10,8},{12,14},{14,12},{16,18},{18,... | collective-permute-start | bytes 776 | tf_op jit(solution)/shard_map/ppermute | solution.py:531
  136.6 3.6 %collective-permute-start.21 = (f32[16,4]{0,1:T(4,128)S(1)}, f32[16,4]{0,1:T(4,128)S(1)}, u32[]{:S(2)}, u32[]{:S(2)}) collective-permute-start(f32[16,4]{0,1:T(4,128)S(1)} %fusion.6), channel_id=1, source_target_pairs={{0,4},{2,6},{4,0},{6,2},{8,12},{10,14},{12,8},{14,10},{16,20},{18,... | collective-permute-start | bytes 776 | tf_op jit(solution)/shard_map/ppermute | solution.py:531
  138.4 4.5 %collective-permute-start.22 = (f32[16,4]{0,1:T(4,128)S(1)}, f32[16,4]{0,1:T(4,128)S(1)}, u32[]{:S(2)}, u32[]{:S(2)}) collective-permute-start(f32[16,4]{0,1:T(4,128)S(1)} %fusion.6), channel_id=1, source_target_pairs={{0,6},{2,4},{4,2},{6,0},{8,14},{10,12},{12,10},{14,8},{16,22},{18,... | collective-permute-start | bytes 776 | tf_op jit(solution)/shard_map/ppermute | solution.py:531
  (13 other events, 24.5 us)

commit v3 on v2

--- a/solution.py
+++ b/solution.py
@@ -14,6 +14,7 @@
 CAP = 4
 PLANES = 4
 CHUNK = 128
+GATE_ROWS = 256
 TILE = 256
 EXTRA = 128
 LOG2E = 1.4426950408889634
@@ -106,7 +107,7 @@
 
 def summary(me, x, b, dt, rate, spread, groups):
     count, length, feats = x.shape
-    width = 512
+    width = 1280
     heads = feats // HEAD_DIM
     piece = (count * NSTATE // groups, feats + EXTRA)
     return pl.pallas_call(
@@ -358,28 +359,30 @@
     def _():
         routed[...] = jnp.zeros_like(routed)
 
-    grow = lane_parts(jnp.exp2(cum[0]), heads)
-    c_out = c[0]
-    square = jnp.zeros((CHUNK, 128), F32)
-    here = slot_pos[...] == row * CHUNK + lax.broadcasted_iota(jnp.int32, (slots, CHUNK), 1)
-    pick = here.astype(F32).astype(BF16)
-    for i in range(feats // TILE):
-        at = pl.ds(i * TILE, TILE)
-        far = mm(c_out, entering[:, at].astype(BF16)) * mm(grow, spread[:, at])
-        half = z[0, :, at].astype(F32) * 0.5
-        value = (y[0, :, at].astype(F32) + far) * (half + half * jnp.tanh(half))
-        kept = (value * gain[:, at]).astype(BF16)
-        gated[0, :, at] = kept
-        power = value * value
-        for j in range(TILE // 128):
-            square = square + power[:, j * 128 : (j + 1) * 128]
-    wide = jnp.broadcast_to(jnp.sum(square, axis=1, keepdims=True), (CHUNK, 128))
-    squares[pl.ds(row, 1), :] = wide.T[0:1, :]
-    hi, mid, lo = three(wide)
-    lane = lax.broadcasted_iota(jnp.int32, (CHUNK, EXTRA), 1)
-    extra = jnp.where(lane == 0, hi, jnp.where(lane == 1, mid, jnp.where(lane == 2, lo, 0.0)))
-    routed[:, pl.ds(0, feats)] += mm(pick, gated[0])
-    routed[:, pl.ds(feats, EXTRA)] += mm(pick, extra.astype(BF16))
+    for sub in range(z.shape[1] // CHUNK):
+        now = pl.ds(sub * CHUNK, CHUNK)
+        line = row * (z.shape[1] // CHUNK) + sub
+        grow = lane_parts(jnp.exp2(cum[0, now, :]), heads)
+        c_out = c[0, now, :]
+        square = jnp.zeros((CHUNK, 128), F32)
+        here = slot_pos[...] == line * CHUNK + lax.broadcasted_iota(jnp.int32, (slots, CHUNK), 1)
+        pick = here.astype(F32).astype(BF16)
+        for i in range(feats // TILE):
+            at = pl.ds(i * TILE, TILE)
+            far = mm(c_out, entering[:, at].astype(BF16)) * mm(grow, spread[:, at])
+            half = z[0, now, at].astype(F32) * 0.5
+            value = (y[0, now, at].astype(F32) + far) * (half + half * jnp.tanh(half))
+            gated[0, now, at] = (value * gain[:, at]).astype(BF16)
+            power = value * value
+            for j in range(TILE // 128):
+                square = square + power[:, j * 128 : (j + 1) * 128]
+        wide = jnp.broadcast_to(jnp.sum(square, axis=1, keepdims=True), (CHUNK, 128))
+        squares[pl.ds(line, 1), :] = wide.T[0:1, :]
+        hi, mid, lo = three(wide)
+        lane = lax.broadcasted_iota(jnp.int32, (CHUNK, EXTRA), 1)
+        extra = jnp.where(lane == 0, hi, jnp.where(lane == 1, mid, jnp.where(lane == 2, lo, 0.0)))
+        routed[:, pl.ds(0, feats)] += mm(pick, gated[0, now, :])
+        routed[:, pl.ds(feats, EXTRA)] += mm(pick, extra.astype(BF16))
 
     @pl.when(row == pl.num_programs(0) * pl.num_programs(1) - 1)
     def _():
@@ -392,14 +395,14 @@
     groups = len(pieces)
     slots = slot_pos.shape[0]
     fixed = lambda shape: pl.BlockSpec(shape, lambda s, i, m: (0,) * len(shape))
-    block = lambda width: pl.BlockSpec((1, CHUNK, width), lambda s, i, m: (s, i, 0))
+    block = lambda width: pl.BlockSpec((1, GATE_ROWS, width), lambda s, i, m: (s, i, 0))
     send = (slots // groups, feats + EXTRA)
     lines = (count * length // CHUNK, 128)
     return pl.pallas_call(
         functools.partial(gate_kernel, groups, feats // HEAD_DIM, slots),
         grid_spec=pltpu.PrefetchScalarGridSpec(
             num_scalar_prefetch=1,
-            grid=(count, length // CHUNK),
+            grid=(count, length // GATE_ROWS),
             in_specs=[fixed(pieces[0].shape)] * groups
             + [block(feats), block(feats), block(NSTATE), block(128)]
             + [fixed((1, feats)), fixed((slots, 1)), pl.BlockSpec(memory_space=pltpu.VMEM)],
@@ -411,7 +414,7 @@
         ),
         out_shape=[jax.ShapeDtypeStruct((count, length, feats), BF16), jax.ShapeDtypeStruct(lines, F32)]
         + [jax.ShapeDtypeStruct(send, BF16)] * groups,
-        compiler_params=pltpu.CompilerParams(vmem_limit_bytes=60 << 20),
+        compiler_params=pltpu.CompilerParams(vmem_limit_bytes=40 << 20),
         cost_estimate=pl.CostEstimate(flops=2_000_000_000, bytes_accessed=20_000_000, transcendentals=0),
         name="gate",
     )(me, *pieces, y, z, c, cum, gain, slot_pos, spread)

time: 145 us -> 137 us (0.945)
  Pallas kernels: 60.8 us -> 55.6 us
  local copies, waits for them, and re-layouts: 14.2 us -> 9.93 us
  waiting for transfers between devices: 27.5 us -> 29.5 us
    pallas_call x1, Pallas kernels: 12.8 us -> 8.71 us  [gate(): pl.pallas_call(functools.partial(gate_kernel, groups, feats // HEAD_DIM,...]
    unnamed x44 -> x38, local copies, waits for them, and re-layouts: 10.3 us -> 8.01 us
    ppermute x20, waiting for transfers between devices: 24.7 us -> 26.8 us  [permute(): return lax.ppermute(value, 'seq', where)]
    pallas_call x1, Pallas kernels: 12.5 us -> 10.5 us  [summary(): pl.pallas_call(functools.partial(summary_kernel, groups, heads), grid_spe...]
  transfers between devices with their start and end apart: 23 -> 23, of which waited for: 12 -> 14; matrix products, arithmetic and copies ran while one was open for 3% -> 1% of each run, Pallas kernels for 23% -> 24%
where the time goes in v3:
time: 137 us; the launch traced here: 136 us
  Pallas kernels  55.6 us (41%)
  starting transfers between devices  37.4 us (27%)
  waiting for transfers between devices  29.5 us (22%)
  local copies, waits for them, and re-layouts  9.93 us (7%)
  other arithmetic  2.91 us (2%)
    ppermute x20, starting transfers between devices, permute(): return lax.ppermute(value, 'seq', where)  37.1 us
    pallas_call x3, Pallas kernels, local_part(): pl.pallas_call(functools.partial(local_kernel, heads, part * feats // HEA...  28.3 us
    ppermute x20, waiting for transfers between devices, permute(): return lax.ppermute(value, 'seq', where)  26.8 us
    pallas_call x1, Pallas kernels, summary(): pl.pallas_call(functools.partial(summary_kernel, groups, heads), grid_spe...  10.5 us
    pallas_call x1, Pallas kernels, gate(): pl.pallas_call(functools.partial(gate_kernel, groups, feats // HEAD_DIM,...  8.71 us
    unnamed x38, local copies, waits for them, and re-layouts  8.01 us
    pallas_call x1, Pallas kernels, scale(): pl.pallas_call(scale_kernel, grid=(count, length // CHUNK), in_specs=[blo...  4.42 us
    ppermute x3, waiting for transfers between devices, swap(): return lax.ppermute(value, 'head', [(0, 1), (1, 0)])  2.78 us
  transfers between devices with their start and end apart: 23, of which 14 were waited for; matrix products, arithmetic and copies ran while one was open for 1% of the time, Pallas kernels for 24%

profile of v3, /device:TPU:0, one launch (start us, length us, event | category | flops | bytes accessed | tf_op | source)
XLA Modules:
  0.0 136.4 jit_solution(9053223687323879477)
XLA Ops:
  1.3 1.4 %fusion.2 = (f32[1,128]{1,0:T(1,128)}, f32[1,128]{1,0:T(1,128)}) fusion(f32[8]{0:T(128)S(1)} %broadcast.86, f32[40]{0:T(128)} %param.20, f32[40]{0:T(128)S(1)} %negate_multiply_fusion), kind=kLoop, calls=%fused_computation.24 | loop fusion | flops 768 | bytes 1376 | tf_op jit(solution)/shard_map/broadcast_in_dim | solution.py:555
  2.8 10.5 %summary.1 = (bf16[64,2688]{1,0:T(8,128)(2,1)}, bf16[64,2688]{1,0:T(8,128)(2,1)}, bf16[64,2688]{1,0:T(8,128)(2,1)}, bf16[64,2688]{1,0:T(8,128)(2,1)}, f32[2,512,128]{2,1,0:T(8,128)}) custom-call(s32[1]{0:T(128)} %bitcast.me, bf16[2,512,2560]{2,1,0:T(8,128)(2,1)} %x.7, bf16[2,512,128]{2,1,0:T(8,128)(2,1)} %b.7, f32[2,40,512]{2,1,0:T(8,128)} %bitcast.25, ...), custom_call_target="tpu_custom_call" | custom-call | flops 2800000000 | bytes 8000000 | tf_op jit(solution)/shard_map/summary/pallas_call | solution.py:113
  13.3 2.9 %collective-permute-start = (bf16[64,2688]{1,0:T(8,128)(2,1)}, bf16[64,2688]{1,0:T(8,128)(2,1)S(1)}, u32[]{:S(2)}, u32[]{:S(2)}) collective-permute-start(bf16[64,2688]{1,0:T(8,128)(2,1)} %get-tuple-element.30), channel_id=1, source_target_pairs={{0,2},{2,0},{4,6},{6,4},{8,10},{10,8},{12,14},{14,12},{16,18},{18,... | collective-permute-start | bytes 1032200 | tf_op jit(solution)/shard_map/ppermute | solution.py:534
  16.2 1.5 %collective-permute-start.1 = (bf16[64,2688]{1,0:T(8,128)(2,1)}, bf16[64,2688]{1,0:T(8,128)(2,1)S(1)}, u32[]{:S(2)}, u32[]{:S(2)}) collective-permute-start(bf16[64,2688]{1,0:T(8,128)(2,1)} %get-tuple-element.31), channel_id=1, source_target_pairs={{0,4},{2,6},{4,0},{6,2},{8,12},{10,14},{12,8},{14,10},{16,20},{18,... | collective-permute-start | bytes 1032200 | tf_op jit(solution)/shard_map/ppermute | solution.py:534
  18.2 12.4 %local_part.3 = (bf16[2,512,2560]{2,1,0:T(8,128)(2,1)}, f32[8,128]{1,0:T(8,128)}) custom-call(bf16[2,512,2560]{2,1,0:T(8,128)(2,1)} %x.7, bf16[2,512,128]{2,1,0:T(8,128)(2,1)} %b.7, bf16[2,512,128]{2,1,0:T(8,128)(2,1)} %refs_6_.1, f32[2,40,512]{2,1,0:T(8,128)} %bitcast.26, f32[1,128]{1,0:T(1,128)} %get-tuple-element.73.rate, ...), custom_call_target="tpu_custom_call" | custom-call | flops 6000000000 | bytes 9000000 | tf_op jit(solution)/shard_map/local_part/pallas_call | solution.py:309
  30.6 2.7 %collective-permute-done.1.rest_2_ = bf16[64,2688]{1,0:T(8,128)(2,1)S(1)} collective-permute-done((bf16[64,2688]{1,0:T(8,128)(2,1)}, bf16[64,2688]{1,0:T(8,128)(2,1)S(1)}, u32[]{:S(2)}, u32[]{:S(2)}) %collective-permute-start.1) | collective-permute-done | bytes 344096 | tf_op jit(solution)/shard_map/ppermute | solution.py:534
  34.5 3.5 %collective-permute-start.3 = (bf16[64,2688]{1,0:T(8,128)(2,1)S(1)}, bf16[64,2688]{1,0:T(8,128)(2,1)S(1)}, u32[]{:S(2)}, u32[]{:S(2)}) collective-permute-start(bf16[64,2688]{1,0:T(8,128)(2,1)S(1)} %plane_total.2.rest_1_), channel_id=1, source_target_pairs={{0,8},{2,10},{4,12},{6,14},{8,16},{10,18},{12,20},{14,22},{16,24},... | collective-permute-start | bytes 1032200 | tf_op jit(solution)/shard_map/ppermute | solution.py:534
  38.0 8.0 %local_part.4 = (bf16[2,512,2560]{2,1,0:T(8,128)(2,1)}, f32[8,128]{1,0:T(8,128)}) custom-call(bf16[2,512,2560]{2,1,0:T(8,128)(2,1)} %x.7, bf16[2,512,128]{2,1,0:T(8,128)(2,1)} %b.7, bf16[2,512,128]{2,1,0:T(8,128)(2,1)} %refs_6_.1, f32[2,40,512]{2,1,0:T(8,128)} %bitcast.27, f32[1,128]{1,0:T(1,128)} %get-tuple-element.73.rate, ...), custom_call_target="tpu_custom_call", output_to_operand_aliasing={{0}: (7, {})} | custom-call | flops 6000000000 | bytes 9000000 | tf_op jit(solution)/shard_map/local_part/pallas_call | solution.py:309
  48.1 4.7 %collective-permute-start.4 = (bf16[64,2688]{1,0:T(8,128)(2,1)S(1)}, bf16[64,2688]{1,0:T(8,128)(2,1)S(1)}, u32[]{:S(2)}, u32[]{:S(2)}) collective-permute-start(bf16[64,2688]{1,0:T(8,128)(2,1)S(1)} %plane_total.3.rest_1_), channel_id=1, source_target_pairs={{0,16},{2,18},{4,20},{6,22},{8,24},{10,26},{12,28},{14,30},{1,17},... | collective-permute-start | bytes 1032200 | tf_op jit(solution)/shard_map/ppermute | solution.py:534
  52.8 8.0 %local_part.5 = (bf16[2,512,2560]{2,1,0:T(8,128)(2,1)}, f32[8,128]{1,0:T(8,128)}) custom-call(bf16[2,512,2560]{2,1,0:T(8,128)(2,1)} %x.7, bf16[2,512,128]{2,1,0:T(8,128)(2,1)} %b.7, bf16[2,512,128]{2,1,0:T(8,128)(2,1)} %refs_6_.1, f32[2,40,512]{2,1,0:T(8,128)} %bitcast.28, f32[1,128]{1,0:T(1,128)} %get-tuple-element.73.rate, ...), custom_call_target="tpu_custom_call", output_to_operand_aliasing={{0}: (7, {})} | custom-call | flops 6000000000 | bytes 9000000 | tf_op jit(solution)/shard_map/local_part/pallas_call | solution.py:309
  61.5 1.6 %incoming_states.1 = (bf16[64,2560]{1,0:T(8,128)(2,1)S(1)}, bf16[64,2560]{1,0:T(8,128)(2,1)}, bf16[64,2560]{1,0:T(8,128)(2,1)}, bf16[64,2560]{1,0:T(8,128)(2,1)}) custom-call(s32[1]{0:T(128)} %bitcast.me, bf16[128,2560]{1,0:T(8,128)(2,1)S(1)} %copy-done.2, bf16[64,2688]{1,0:T(8,128)(2,1)S(1)} %copy-done.5, ...), custom_call_target="tpu_custom_call" | custom-call | flops 10000000 | bytes 2500000 | tf_op jit(solution)/shard_map/incoming_states/pallas_call | solution.py:228
  63.1 1.2 collective-permute-start.5
  65.2 1.4 %collective-permute-start.7 = (bf16[64,2560]{1,0:T(8,128)(2,1)}, bf16[64,2560]{1,0:T(8,128)(2,1)S(1)}, u32[]{:S(2)}, u32[]{:S(2)}) collective-permute-start(bf16[64,2560]{1,0:T(8,128)(2,1)} %get-tuple-element.41), channel_id=1, source_target_pairs={{0,6},{2,4},{4,2},{6,0},{8,14},{10,12},{12,10},{14,8},{16,22},{18,... | collective-permute-start | bytes 983048 | tf_op jit(solution)/shard_map/ppermute | solution.py:534
  66.8 7.1 %collective-permute-done.5.refs_1_ = bf16[64,2560]{1,0:T(8,128)(2,1)S(1)} collective-permute-done((bf16[64,2560]{1,0:T(8,128)(2,1)}, bf16[64,2560]{1,0:T(8,128)(2,1)S(1)}, u32[]{:S(2)}, u32[]{:S(2)}) %collective-permute-start.5) | collective-permute-done | bytes 327712 | tf_op jit(solution)/shard_map/ppermute | solution.py:534
  74.0 5.3 %collective-permute-done.6.refs_2_ = bf16[64,2560]{1,0:T(8,128)(2,1)S(1)} collective-permute-done((bf16[64,2560]{1,0:T(8,128)(2,1)}, bf16[64,2560]{1,0:T(8,128)(2,1)S(1)}, u32[]{:S(2)}, u32[]{:S(2)}) %collective-permute-start.6) | collective-permute-done | bytes 327712 | tf_op jit(solution)/shard_map/ppermute | solution.py:534
  79.3 2.5 %copy-done.3 = bf16[2,512,2560]{2,1,0:T(8,128)(2,1)S(1)} copy-done((bf16[2,512,2560]{2,1,0:T(8,128)(2,1)S(1)}, bf16[2,512,2560]{2,1,0:T(8,128)(2,1)}, u32[]{:S(2)}) %copy-start.3) | copy-done | bytes 5242904
  81.8 8.7 %gate.1 = (bf16[2,512,2560]{2,1,0:T(8,128)(2,1)S(1)}, f32[8,128]{1,0:T(8,128)S(1)}, bf16[16,2688]{1,0:T(8,128)(2,1)S(1)}, bf16[16,2688]{1,0:T(8,128)(2,1)S(1)}, ...) custom-call(s32[1]{0:T(128)} %bitcast.me, bf16[64,2560]{1,0:T(8,128)(2,1)S(1)} %get-tuple-element.38.refs_0_, ...), custom_call_target="tpu_custom_call" | custom-call | flops 2000000000 | bytes 20000000 | tf_op jit(solution)/shard_map/gate/pallas_call | solution.py:401
  91.2 1.2 collective-permute-start.10
  92.3 1.8 %collective-permute-start.11 = (bf16[16,2688]{1,0:T(8,128)(2,1)S(1)}, bf16[16,2688]{1,0:T(8,128)(2,1)S(1)}, u32[]{:S(2)}, u32[]{:S(2)}) collective-permute-start(bf16[16,2688]{1,0:T(8,128)(2,1)S(1)} %get-tuple-element.49), channel_id=1, source_target_pairs={{0,6},{2,4},{4,2},{6,0},{8,14},{10,12},{12,10},{14,8},{16,22},{18,... | collective-permute-start | bytes 258056 | tf_op jit(solution)/shard_map/ppermute | solution.py:534
  95.7 2.0 %collective-permute-done.11 = bf16[16,2688]{1,0:T(8,128)(2,1)S(1)} collective-permute-done((bf16[16,2688]{1,0:T(8,128)(2,1)S(1)}, bf16[16,2688]{1,0:T(8,128)(2,1)S(1)}, u32[]{:S(2)}, u32[]{:S(2)}) %collective-permute-start.11) | collective-permute-done | bytes 86048 | tf_op jit(solution)/shard_map/ppermute | solution.py:534
  97.8 8.8 %collective-permute-start.14 = (bf16[16,2688]{1,0:T(8,128)(2,1)S(1)}, bf16[16,2688]{1,0:T(8,128)(2,1)S(1)}, u32[]{:S(2)}, u32[]{:S(2)}) collective-permute-start(bf16[16,2688]{1,0:T(8,128)(2,1)S(1)} %pad_maximum_fusion.3), channel_id=1, source_target_pairs={{0,24},{2,26},{4,28},{6,30},{8,16},{10,18},{12,20},{14,22},{16,8},... | collective-permute-start | bytes 258056 | tf_op jit(solution)/shard_map/ppermute | solution.py:534
  107.5 4.4 %scale.1 = (bf16[2,512,2560]{2,1,0:T(8,128)(2,1)}, f32[8,128]{1,0:T(8,128)S(1)}) custom-call(bf16[2,512,2560]{2,1,0:T(8,128)(2,1)S(1)} %get-tuple-element.44.gated, f32[8,128]{1,0:T(8,128)S(1)} %get-tuple-element.45.mine, f32[8,128]{1,0:T(8,128)S(1)} %collective-permute-done.8.other, bf16[16,2688]{1,0:T(8,128)(2,1)S(1)} %pad_maximum_fusion.rest_0_), custom_call_target="tpu_custom_call" | custom-call | flops 10000000 | bytes 8000000 | tf_op jit(solution)/shard_map/scale/pallas_call | solution.py:438
  112.4 1.6 %collective-permute-done.15.other = bf16[64,2688]{1,0:T(8,128)(2,1)S(1)} collective-permute-done((bf16[64,2688]{1,0:T(8,128)(2,1)S(1)}, bf16[64,2688]{1,0:T(8,128)(2,1)S(1)}, u32[]{:S(2)}, u32[]{:S(2)}) %collective-permute-start.15) | collective-permute-done | bytes 344096 | tf_op jit(solution)/shard_map/ppermute | solution.py:540
  114.1 2.5 %copy-done.4 = bf16[1,5120,512]{2,1,0:T(8,128)(2,1)S(1)} copy-done((bf16[1,5120,512]{2,1,0:T(8,128)(2,1)S(1)}, bf16[1,5120,512]{2,1,0:T(8,128)(2,1)}, u32[]{:S(2)}) %copy-start.4) | copy-done | bytes 5242904
  116.5 1.1 expert.1
  117.7 1.1 collective-permute-start.16
  118.8 2.9 %collective-permute-start.17 = (f32[16,1]{1,0:T(8,128)S(1)}, f32[16,1]{1,0:T(8,128)S(1)}, u32[]{:S(2)}, u32[]{:S(2)}) collective-permute-start(f32[16,1]{1,0:T(8,128)S(1)} %bitcast.22), channel_id=1, source_target_pairs={{0,16},{2,18},{4,20},{6,22},{8,24},{10,26},{12,28},{14,30},{16,0},... | collective-permute-start | bytes 200 | tf_op jit(solution)/shard_map/ppermute | solution.py:534
  123.4 3.7 %collective-permute-done.18 = f32[16,1]{1,0:T(8,128)S(1)} collective-permute-done((f32[16,1]{1,0:T(8,128)S(1)}, f32[16,1]{1,0:T(8,128)S(1)}, u32[]{:S(2)}, u32[]{:S(2)}) %collective-permute-start.18) | collective-permute-done | bytes 96 | tf_op jit(solution)/shard_map/ppermute | solution.py:534
  127.3 1.1 collective-permute-done.19
  129.1 1.7 %collective-permute-start.21 = (f32[16,4]{0,1:T(4,128)S(1)}, f32[16,4]{0,1:T(4,128)S(1)}, u32[]{:S(2)}, u32[]{:S(2)}) collective-permute-start(f32[16,4]{0,1:T(4,128)S(1)} %fusion.6), channel_id=1, source_target_pairs={{0,4},{2,6},{4,0},{6,2},{8,12},{10,14},{12,8},{14,10},{16,20},{18,... | collective-permute-start | bytes 776 | tf_op jit(solution)/shard_map/ppermute | solution.py:534
  130.9 1.2 collective-permute-start.22
  133.0 2.4 %collective-permute-done.22 = f32[16,4]{0,1:T(4,128)S(1)} collective-permute-done((f32[16,4]{0,1:T(4,128)S(1)}, f32[16,4]{0,1:T(4,128)S(1)}, u32[]{:S(2)}, u32[]{:S(2)}) %collective-permute-start.22) | collective-permute-done | bytes 288 | tf_op jit(solution)/shard_map/ppermute | solution.py:534
  (100 shorter events, 14.1 us)
Async XLA Ops:
  0.6 17.1 %copy-start.18 = (s32[2,32]{1,0:T(2,128)S(1)}, s32[2,32]{1,0:T(2,128)}, u32[]{:S(2)}) copy-start(s32[2,32]{1,0:T(2,128)} %param.23) | copy-start | bytes 772
  0.6 17.4 %copy-start.17 = (s32[2,32]{1,0:T(2,128)S(1)}, s32[2,32]{1,0:T(2,128)}, u32[]{:S(2)}) copy-start(s32[2,32]{1,0:T(2,128)} %param.22) | copy-start | bytes 772
  13.3 17.3 %collective-permute-start = (bf16[64,2688]{1,0:T(8,128)(2,1)}, bf16[64,2688]{1,0:T(8,128)(2,1)S(1)}, u32[]{:S(2)}, u32[]{:S(2)}) collective-permute-start(bf16[64,2688]{1,0:T(8,128)(2,1)} %get-tuple-element.30), channel_id=1, source_target_pairs={{0,2},{2,0},{4,6},{6,4},{8,10},{10,8},{12,14},{14,12},{16,18},{18,... | collective-permute-start | bytes 1032200 | tf_op jit(solution)/shard_map/ppermute | solution.py:534
  16.2 17.1 %collective-permute-start.1 = (bf16[64,2688]{1,0:T(8,128)(2,1)}, bf16[64,2688]{1,0:T(8,128)(2,1)S(1)}, u32[]{:S(2)}, u32[]{:S(2)}) collective-permute-start(bf16[64,2688]{1,0:T(8,128)(2,1)} %get-tuple-element.31), channel_id=1, source_target_pairs={{0,4},{2,6},{4,0},{6,2},{8,12},{10,14},{12,8},{14,10},{16,20},{18,... | collective-permute-start | bytes 1032200 | tf_op jit(solution)/shard_map/ppermute | solution.py:534
  17.7 15.6 %collective-permute-start.2 = (bf16[64,2688]{1,0:T(8,128)(2,1)}, bf16[64,2688]{1,0:T(8,128)(2,1)S(1)}, u32[]{:S(2)}, u32[]{:S(2)}) collective-permute-start(bf16[64,2688]{1,0:T(8,128)(2,1)} %get-tuple-element.32), channel_id=1, source_target_pairs={{0,6},{2,4},{4,2},{6,0},{8,14},{10,12},{12,10},{14,8},{16,22},{18,... | collective-permute-start | bytes 1032200 | tf_op jit(solution)/shard_map/ppermute | solution.py:534
  18.2 15.1 %copy-start = (bf16[128,2560]{1,0:T(8,128)(2,1)S(1)}, bf16[128,2560]{1,0:T(8,128)(2,1)}, u32[]{:S(2)}) copy-start(bf16[128,2560]{1,0:T(8,128)(2,1)} %constant.68.clone.spread.refs_10_) | copy-start | bytes 1966084
  18.2 15.1 %copy-start.5 = (bf16[64,2688]{1,0:T(8,128)(2,1)S(1)}, bf16[64,2688]{1,0:T(8,128)(2,1)}, u32[]{:S(2)}) copy-start(bf16[64,2688]{1,0:T(8,128)(2,1)} %get-tuple-element.29.rest_0_) | copy-start | bytes 1032196
  34.5 11.5 %collective-permute-start.3 = (bf16[64,2688]{1,0:T(8,128)(2,1)S(1)}, bf16[64,2688]{1,0:T(8,128)(2,1)S(1)}, u32[]{:S(2)}, u32[]{:S(2)}) collective-permute-start(bf16[64,2688]{1,0:T(8,128)(2,1)S(1)} %plane_total.2.rest_1_), channel_id=1, source_target_pairs={{0,8},{2,10},{4,12},{6,14},{8,16},{10,18},{12,20},{14,22},{16,24},... | collective-permute-start | bytes 1032200 | tf_op jit(solution)/shard_map/ppermute | solution.py:534
  48.1 12.7 %collective-permute-start.4 = (bf16[64,2688]{1,0:T(8,128)(2,1)S(1)}, bf16[64,2688]{1,0:T(8,128)(2,1)S(1)}, u32[]{:S(2)}, u32[]{:S(2)}) collective-permute-start(bf16[64,2688]{1,0:T(8,128)(2,1)S(1)} %plane_total.3.rest_1_), channel_id=1, source_target_pairs={{0,16},{2,18},{4,20},{6,22},{8,24},{10,26},{12,28},{14,30},{1,17},... | collective-permute-start | bytes 1032200 | tf_op jit(solution)/shard_map/ppermute | solution.py:534
  52.8 14.1 %copy-start.16 = (f32[2560]{0:T(1024)S(1)}, f32[2560]{0:T(1024)}, u32[]{:S(2)}) copy-start(f32[2560]{0:T(1024)} %param.21) | copy-start | bytes 30724
  52.8 26.5 %copy-start.8 = (f32[2,512,128]{2,1,0:T(8,128)S(1)}, f32[2,512,128]{2,1,0:T(8,128)}, u32[]{:S(2)}) copy-start(f32[2,512,128]{2,1,0:T(8,128)} %get-tuple-element.43.refs_7_) | copy-start | bytes 1572868
  52.8 26.5 %copy-start.10 = (bf16[2,512,128]{2,1,0:T(8,128)(2,1)S(1)}, bf16[2,512,128]{2,1,0:T(8,128)(2,1)}, u32[]{:S(2)}) copy-start(bf16[2,512,128]{2,1,0:T(8,128)(2,1)} %refs_6_.1) | copy-start | bytes 786436
  63.1 10.9 %collective-permute-start.5 = (bf16[64,2560]{1,0:T(8,128)(2,1)}, bf16[64,2560]{1,0:T(8,128)(2,1)S(1)}, u32[]{:S(2)}, u32[]{:S(2)}) collective-permute-start(bf16[64,2560]{1,0:T(8,128)(2,1)} %get-tuple-element.39), channel_id=1, source_target_pairs={{0,2},{2,0},{4,6},{6,4},{8,10},{10,8},{12,14},{14,12},{16,18},{18,... | collective-permute-start | bytes 983048 | tf_op jit(solution)/shard_map/ppermute | solution.py:534
  64.3 15.0 %collective-permute-start.6 = (bf16[64,2560]{1,0:T(8,128)(2,1)}, bf16[64,2560]{1,0:T(8,128)(2,1)S(1)}, u32[]{:S(2)}, u32[]{:S(2)}) collective-permute-start(bf16[64,2560]{1,0:T(8,128)(2,1)} %get-tuple-element.40), channel_id=1, source_target_pairs={{0,4},{2,6},{4,0},{6,2},{8,12},{10,14},{12,8},{14,10},{16,20},{18,... | collective-permute-start | bytes 983048 | tf_op jit(solution)/shard_map/ppermute | solution.py:534
  65.2 14.1 %collective-permute-start.7 = (bf16[64,2560]{1,0:T(8,128)(2,1)}, bf16[64,2560]{1,0:T(8,128)(2,1)S(1)}, u32[]{:S(2)}, u32[]{:S(2)}) collective-permute-start(bf16[64,2560]{1,0:T(8,128)(2,1)} %get-tuple-element.41), channel_id=1, source_target_pairs={{0,6},{2,4},{4,2},{6,0},{8,14},{10,12},{12,10},{14,8},{16,22},{18,... | collective-permute-start | bytes 983048 | tf_op jit(solution)/shard_map/ppermute | solution.py:534
  90.5 23.5 %copy-start.14 = (f32[1,512]{1,0:T(1,128)S(1)}, f32[1,512]{1,0:T(1,128)}, u32[]{:S(2)}) copy-start(f32[1,512]{1,0:T(1,128)} %b1.1) | copy-start | bytes 6148
  90.5 23.5 %copy-start.15 = (bf16[1,512]{1,0:T(2,128)(2,1)S(1)}, bf16[1,512]{1,0:T(2,128)(2,1)}, u32[]{:S(2)}) copy-start(bf16[1,512]{1,0:T(2,128)(2,1)} %w2.1) | copy-start | bytes 3076
  90.5 4.6 %collective-permute-start.9 = (bf16[16,2688]{1,0:T(8,128)(2,1)S(1)}, bf16[16,2688]{1,0:T(8,128)(2,1)S(1)}, u32[]{:S(2)}, u32[]{:S(2)}) collective-permute-start(bf16[16,2688]{1,0:T(8,128)(2,1)S(1)} %get-tuple-element.47), channel_id=1, source_target_pairs={{0,2},{2,0},{4,6},{6,4},{8,10},{10,8},{12,14},{14,12},{16,18},{18,... | collective-permute-start | bytes 258056 | tf_op jit(solution)/shard_map/ppermute | solution.py:534
  91.2 4.5 %collective-permute-start.10 = (bf16[16,2688]{1,0:T(8,128)(2,1)S(1)}, bf16[16,2688]{1,0:T(8,128)(2,1)S(1)}, u32[]{:S(2)}, u32[]{:S(2)}) collective-permute-start(bf16[16,2688]{1,0:T(8,128)(2,1)S(1)} %get-tuple-element.48), channel_id=1, source_target_pairs={{0,4},{2,6},{4,0},{6,2},{8,12},{10,14},{12,8},{14,10},{16,20},{18,... | collective-permute-start | bytes 258056 | tf_op jit(solution)/shard_map/ppermute | solution.py:534
  92.3 5.4 %collective-permute-start.11 = (bf16[16,2688]{1,0:T(8,128)(2,1)S(1)}, bf16[16,2688]{1,0:T(8,128)(2,1)S(1)}, u32[]{:S(2)}, u32[]{:S(2)}) collective-permute-start(bf16[16,2688]{1,0:T(8,128)(2,1)S(1)} %get-tuple-element.49), channel_id=1, source_target_pairs={{0,6},{2,4},{4,2},{6,0},{8,14},{10,12},{12,10},{14,8},{16,22},{18,... | collective-permute-start | bytes 258056 | tf_op jit(solution)/shard_map/ppermute | solution.py:534
  94.1 13.4 %collective-permute-start.8 = (f32[8,128]{1,0:T(8,128)S(1)}, f32[8,128]{1,0:T(8,128)S(1)}, u32[]{:S(2)}, u32[]{:S(2)}) collective-permute-start(f32[8,128]{1,0:T(8,128)S(1)} %get-tuple-element.45.mine), channel_id=1, source_target_pairs={{0,1},{1,0},{2,3},{3,2},{4,5},{5,4},{6,7},{7,6},{8,9},{9,8},{10,11... | collective-permute-start | bytes 12296 | tf_op jit(solution)/shard_map/ppermute | solution.py:540
  97.8 14.1 %collective-permute-start.14 = (bf16[16,2688]{1,0:T(8,128)(2,1)S(1)}, bf16[16,2688]{1,0:T(8,128)(2,1)S(1)}, u32[]{:S(2)}, u32[]{:S(2)}) collective-permute-start(bf16[16,2688]{1,0:T(8,128)(2,1)S(1)} %pad_maximum_fusion.3), channel_id=1, source_target_pairs={{0,24},{2,26},{4,28},{6,30},{8,16},{10,18},{12,20},{14,22},{16,8},... | collective-permute-start | bytes 258056 | tf_op jit(solution)/shard_map/ppermute | solution.py:534
  106.7 5.6 %collective-permute-start.13 = (bf16[16,2688]{1,0:T(8,128)(2,1)S(1)}, bf16[16,2688]{1,0:T(8,128)(2,1)S(1)}, u32[]{:S(2)}, u32[]{:S(2)}) collective-permute-start(bf16[16,2688]{1,0:T(8,128)(2,1)S(1)} %pad_maximum_fusion.2), channel_id=1, source_target_pairs={{0,16},{2,18},{4,20},{6,22},{8,24},{10,26},{12,28},{14,30},{16,0},... | collective-permute-start | bytes 258056 | tf_op jit(solution)/shard_map/ppermute | solution.py:534
  106.8 5.5 %collective-permute-start.12 = (bf16[16,2688]{1,0:T(8,128)(2,1)S(1)}, bf16[16,2688]{1,0:T(8,128)(2,1)S(1)}, u32[]{:S(2)}, u32[]{:S(2)}) collective-permute-start(bf16[16,2688]{1,0:T(8,128)(2,1)S(1)} %pad_maximum_fusion.rest_0_), channel_id=1, source_target_pairs={{0,8},{2,10},{4,12},{6,14},{8,0},{10,2},{12,4},{14,6},{16,24},{18,... | collective-permute-start | bytes 258056 | tf_op jit(solution)/shard_map/ppermute | solution.py:534
  112.3 1.7 %collective-permute-start.15 = (bf16[64,2688]{1,0:T(8,128)(2,1)S(1)}, bf16[64,2688]{1,0:T(8,128)(2,1)S(1)}, u32[]{:S(2)}, u32[]{:S(2)}) collective-permute-start(bf16[64,2688]{1,0:T(8,128)(2,1)S(1)} %join.1.own), channel_id=1, source_target_pairs={{0,1},{1,0},{2,3},{3,2},{4,5},{5,4},{6,7},{7,6},{8,9},{9,8},{10,11... | collective-permute-start | bytes 1032200 | tf_op jit(solution)/shard_map/ppermute | solution.py:540
  117.7 4.5 %collective-permute-start.16 = (f32[16,1]{1,0:T(8,128)S(1)}, f32[16,1]{1,0:T(8,128)S(1)}, u32[]{:S(2)}, u32[]{:S(2)}) collective-permute-start(f32[16,1]{1,0:T(8,128)S(1)} %bitcast.23), channel_id=1, source_target_pairs={{0,8},{2,10},{4,12},{6,14},{8,0},{10,2},{12,4},{14,6},{16,24},{18,... | collective-permute-start | bytes 200 | tf_op jit(solution)/shard_map/ppermute | solution.py:534
  118.8 4.5 %collective-permute-start.17 = (f32[16,1]{1,0:T(8,128)S(1)}, f32[16,1]{1,0:T(8,128)S(1)}, u32[]{:S(2)}, u32[]{:S(2)}) collective-permute-start(f32[16,1]{1,0:T(8,128)S(1)} %bitcast.22), channel_id=1, source_target_pairs={{0,16},{2,18},{4,20},{6,22},{8,24},{10,26},{12,28},{14,30},{16,0},... | collective-permute-start | bytes 200 | tf_op jit(solution)/shard_map/ppermute | solution.py:534
  121.7 5.4 %collective-permute-start.18 = (f32[16,1]{1,0:T(8,128)S(1)}, f32[16,1]{1,0:T(8,128)S(1)}, u32[]{:S(2)}, u32[]{:S(2)}) collective-permute-start(f32[16,1]{1,0:T(8,128)S(1)} %bitcast.21), channel_id=1, source_target_pairs={{0,24},{2,26},{4,28},{6,30},{8,16},{10,18},{12,20},{14,22},{16,8},... | collective-permute-start | bytes 200 | tf_op jit(solution)/shard_map/ppermute | solution.py:534
  127.3 1.2 collective-permute-start.19
  128.5 3.7 %collective-permute-start.20 = (f32[16,4]{0,1:T(4,128)S(1)}, f32[16,4]{0,1:T(4,128)S(1)}, u32[]{:S(2)}, u32[]{:S(2)}) collective-permute-start(f32[16,4]{0,1:T(4,128)S(1)} %fusion.6), channel_id=1, source_target_pairs={{0,2},{2,0},{4,6},{6,4},{8,10},{10,8},{12,14},{14,12},{16,18},{18,... | collective-permute-start | bytes 776 | tf_op jit(solution)/shard_map/ppermute | solution.py:534
  129.1 3.6 %collective-permute-start.21 = (f32[16,4]{0,1:T(4,128)S(1)}, f32[16,4]{0,1:T(4,128)S(1)}, u32[]{:S(2)}, u32[]{:S(2)}) collective-permute-start(f32[16,4]{0,1:T(4,128)S(1)} %fusion.6), channel_id=1, source_target_pairs={{0,4},{2,6},{4,0},{6,2},{8,12},{10,14},{12,8},{14,10},{16,20},{18,... | collective-permute-start | bytes 776 | tf_op jit(solution)/shard_map/ppermute | solution.py:534
  130.9 4.5 %collective-permute-start.22 = (f32[16,4]{0,1:T(4,128)S(1)}, f32[16,4]{0,1:T(4,128)S(1)}, u32[]{:S(2)}, u32[]{:S(2)}) collective-permute-start(f32[16,4]{0,1:T(4,128)S(1)} %fusion.6), channel_id=1, source_target_pairs={{0,6},{2,4},{4,2},{6,0},{8,14},{10,12},{12,10},{14,8},{16,22},{18,... | collective-permute-start | bytes 776 | tf_op jit(solution)/shard_map/ppermute | solution.py:534
  (10 other events, 32.2 us)
